TPU v7x, 32 devices: a whole 2x2x4 slice. The times are simulated.
32 devices in a mesh: dp: 8 (over z, y), tensor: 4 (over x, core).
Axes of the slice: x: 2, y: 2, z: 4, core: 2. Of those that a mesh axis runs over, the one named last changes fastest.
Arguments:
- block_input: bfloat16 [8192, 768], P(('dp', 'tensor')), may hold values from -6 to 6
- output_grad: bfloat16 [8192, 768], P(('dp', 'tensor')), may hold values from -6 to 6
- segment_ids: int32 [8, 1024], P('dp'), may hold values from 0 to 3, as said below
- positions: int32 [8, 1024], P('dp'), may hold values from 0 to 639, as said below
- gain_one: float32 [768], replicated, may hold values from 0.5 to 1.5
- gain_two: float32 [768], replicated, may hold values from 0.5 to 1.5
- qkv_weight: bfloat16 [768, 3, 768], P(None, None, 'tensor')
- proj_weight: bfloat16 [768, 768], P('tensor'), may hold values from -0.875 to 0.875
- wide_weight: bfloat16 [768, 2, 1152], P(None, None, 'tensor'), may hold values from -0.21875 to 0.21875
- down_weight: bfloat16 [1152, 768], P('tensor'), may hold values from -0.1875 to 0.1875
Outputs:
- block_output: bfloat16 [8192, 768], P(('dp', 'tensor'))
- grad_input: float32 [8192, 768], P(('dp', 'tensor'))
- grad_qkv: float32 [768, 3, 768], P('dp', None, 'tensor')
- grad_proj: float32 [768, 768], P('tensor', 'dp')
- grad_wide: float32 [768, 2, 1152], P('dp', None, 'tensor')
- grad_down: float32 [1152, 768], P('tensor', 'dp')
- grad_gains: float32 [2, 768], replicated
Inputs may be any that keep to these rules, and one draw needn't show every extreme that they name: `segment_ids`: in each row the ids never fall and name 4 documents, each of 128 positions or more; some row has a document of 1024 - 3 * (128) positions. `positions`: each token's place within its document: 0 at a document's first token, rising by one.
All inputs are finite; a program needn't handle non-finite values.
Results may differ from a plain program's by a relative error of at most 0.014.
Values may be sent and summed in bfloat16 or wider, within the bound.
No kernel may reach another device: no remote copies, remote signals or barrier semaphores. Data moves between devices by JAX's collectives and lax.ppermute only.
A program may use at most 128 MiB of HBM per device.

v0:
```python
import functools
import math

import jax
import jax.numpy as jnp
from jax import lax
from jax.experimental import pallas as pl
from jax.experimental.pallas import tpu as pltpu
from jax.sharding import PartitionSpec as P


HD = 64


NORM_EPSILON = 1e-05
ROPE_THETA = 160000.0
MASK_FLOOR = -1e30
TILE = 256
LOW = jnp.bfloat16
WIDE = jnp.float32


def bits_of(axis):
    return range(int(math.log2(lax.axis_size(axis))))


def swap(values_in, axis, bit):
    size = lax.axis_size(axis)
    return lax.ppermute(values_in, axis, [(i, i ^ (1 << bit)) for i in range(size)])


def sum_everywhere(values_in):
    steps = [("dp", bit) for bit in bits_of("dp")]
    steps[1:1] = [("tensor", 0)]
    steps += [("tensor", bit) for bit in bits_of("tensor") if bit]
    for axis, bit in steps:
        values_in = values_in + swap(values_in, axis, bit)
    return values_in


def scatter_rows(kept, away, order):
    left = sorted(order, reverse=True)
    for step, bit in enumerate(order):
        axis = left.index(bit)
        if step:
            total = total.reshape((2,) * len(left) + kept.shape[-2:])
            away = lax.index_in_dim(total, 1, axis, keepdims=False).astype(LOW)
            kept = lax.index_in_dim(total, 0, axis, keepdims=False)
        came = swap(away, "dp", bit)
        left.remove(bit)
        if left:
            total = kept + came.astype(WIDE)
    return kept.reshape(kept.shape[-2:]), came.reshape(kept.shape[-2:])


def call(kernel, outs, *operands, scalars=0, flops=0, scratch=(), limit=20, streamed=False):
    spaces = [pl.BlockSpec(memory_space=pltpu.SMEM)] * scalars
    space = pltpu.HBM if streamed else pltpu.VMEM
    spaces += [pl.BlockSpec(memory_space=space)] * (len(operands) - scalars)
    held = [pltpu.VMEM(shape, kind) for shape, kind in scratch]
    if streamed:
        held += [pltpu.VMEM(x.shape, x.dtype) for x in operands[scalars:]]
        held += [pltpu.SemaphoreType.DMA((len(operands) - scalars,))]
    moved = sum(x.size * x.dtype.itemsize for x in operands)
    shapes = [jax.ShapeDtypeStruct(shape, kind) for shape, kind in outs]
    return pl.pallas_call(
        kernel,
        out_shape=shapes,
        in_specs=spaces,
        out_specs=[pl.BlockSpec(memory_space=pltpu.VMEM)] * len(shapes),
        scratch_shapes=held,
        compiler_params=pltpu.CompilerParams(vmem_limit_bytes=limit << 20),
        cost_estimate=pl.CostEstimate(flops=flops, bytes_accessed=moved, transcendentals=0),
    )(*operands)


def dot(left, right, left_axis=1, right_axis=0):
    return lax.dot_general(
        left, right, (((left_axis,), (right_axis,)), ((), ())), preferred_element_type=WIDE
    )


def normalise(values_in):
    average = jnp.mean(values_in, axis=-1, keepdims=True)
    centred = values_in - average
    spread = jnp.mean(centred * centred, axis=-1, keepdims=True)
    scale = lax.rsqrt(spread + NORM_EPSILON)
    return centred * scale, scale


def normalise_back(grads_in, hat, scale, gain_in):
    scaled = grads_in * gain_in
    first = jnp.mean(scaled, axis=-1, keepdims=True)
    second = jnp.mean(scaled * hat, axis=-1, keepdims=True)
    return scale * (scaled - first - hat * second)


def prepare_kernel(own_ref, segment_ref, places_ref, row_ref, column_ref, cos_ref, sin_ref, *, count):
    half = cos_ref.shape[0]
    rows = row_ref.shape[1] // count
    step = lax.broadcasted_iota(jnp.int32, (half, rows), 0).astype(WIDE)
    inverse = jnp.exp(step * (-math.log(ROPE_THETA) / half))
    for place in range(count):
        start = pl.multiple_of(jnp.bitwise_xor(own_ref[0], place) * rows, rows)
        at = slice(place * rows, (place + 1) * rows)
        segment = segment_ref[:, pl.ds(start, rows)]
        row_ref[:, at] = segment
        column_ref[at, :] = jnp.broadcast_to(segment, (column_ref.shape[1], rows)).T
        angles = inverse * places_ref[:, pl.ds(start, rows)].astype(WIDE)
        cos_ref[:, at] = jnp.cos(angles)
        sin_ref[:, at] = jnp.sin(angles)


def qkv_kernel(
    near_ref, far_ref, gain_ref, turned_ref, cos_ref, sin_ref, turned_normed_ref, normed_ref, out_ref,
    *, offset
):
    rows = near_ref.shape[0]
    half = HD // 2
    heads = turned_ref.shape[0] // (3 * HD)
    for place, ref in enumerate((near_ref, far_ref)):
        at = slice(place * rows, (place + 1) * rows)
        hat, _ = normalise(ref[...].astype(WIDE))
        normed = (hat * gain_ref[...]).astype(LOW)
        normed_ref[at, :] = normed
        turned_normed_ref[:, at] = normed.T
        mixed = dot(turned_ref[...], normed, 1, 1)
        there = slice(offset + place * rows, offset + (place + 1) * rows)
        cosine, sine = cos_ref[:, there], sin_ref[:, there]
        for head in range(2 * heads):
            lower = mixed[head * HD : head * HD + half]
            upper = mixed[head * HD + half : (head + 1) * HD]
            scale = 1.0 / math.sqrt(HD) if head < heads else 1.0
            first = (lower * cosine - upper * sine).astype(LOW)
            second = (upper * cosine + lower * sine).astype(LOW)
            out_ref[head * HD : head * HD + half, at] = first * scale
            out_ref[head * HD + half : (head + 1) * HD, at] = second * scale
        out_ref[2 * heads * HD :, at] = mixed[2 * heads * HD :].astype(LOW)


def attend_kernel(
    near_ref, far_ref, seg_row_ref, seg_col_ref, proj_ref,
    out_ref, total_ref, keep_near_ref, keep_far_ref, away_near_ref, away_far_ref,
    keys_ref, values_ref,
):
    length = seg_row_ref.shape[1]
    half_length = near_ref.shape[1]
    width = proj_ref.shape[0]
    heads = width // HD
    for place, ref in enumerate((near_ref, far_ref)):
        at = slice(place * half_length, (place + 1) * half_length)
        for head in range(heads):
            keys = ref[width + head * HD : width + (head + 1) * HD, :]
            keys_ref[head, at, :] = keys.T
        values_ref[:, at] = ref[2 * width :, :]
    for tile in range(length // TILE):
        ref = near_ref if tile * TILE < half_length else far_ref
        first = (tile * TILE) % half_length
        at = slice(tile * TILE, (tile + 1) * TILE)
        column = jnp.concatenate([seg_col_ref[...]] * (TILE // seg_col_ref.shape[1]), 1)
        same = column == seg_row_ref[:, at]
        for head in range(heads):
            query = ref[head * HD : (head + 1) * HD, first : first + TILE]
            scores = jnp.where(same, dot(keys_ref[head], query), MASK_FLOOR)
            top = jnp.max(scores, 0, keepdims=True)
            raised = jnp.exp(scores - top)
            total = jnp.sum(raised, 0, keepdims=True)
            mixed = dot(values_ref[head * HD : (head + 1) * HD, :], raised.astype(LOW))
            out_ref[head * HD : (head + 1) * HD, at] = (mixed / total).astype(LOW)
            total_ref[head, :, at] = top + jnp.log(total)
    rows = keep_near_ref.shape[0]
    refs = (keep_near_ref, away_near_ref, keep_far_ref, away_far_ref)
    for place, ref in enumerate(refs):
        part = dot(out_ref[:, place * rows : (place + 1) * rows], proj_ref[...], 0, 0)
        ref[...] = part.astype(ref.dtype)


def middle_kernel(x_ref, keep_ref, core_ref, chip_ref, gain_ref, mid_ref, normed_ref):
    total = x_ref[...].astype(WIDE) + keep_ref[...]
    total = total + core_ref[...].astype(WIDE) + chip_ref[...].astype(WIDE)
    mid_ref[...] = total
    normed_ref[...] = (normalise(total)[0] * gain_ref[...]).astype(LOW)


def forward_kernel(
    near_ref, far_ref, grad_near_ref, grad_far_ref, gate_w_ref, up_w_ref, down_ref,
    dgate_ref, dup_ref, act_ref, keep_ref, away_ref, gain_ref,
):
    gain_total = None
    rows = near_ref.shape[0]
    parts = ((near_ref, grad_near_ref, keep_ref), (far_ref, grad_far_ref, away_ref))
    for place, (ref, grad_ref, part_ref) in enumerate(parts):
        at = slice(place * rows, (place + 1) * rows)
        gate = dot(ref[...], gate_w_ref[...], 1, 1)
        up = dot(ref[...], up_w_ref[...], 1, 1)
        grad_act = dot(grad_ref[...], down_ref[...], 1, 1)
        share = 0.5 * (1.0 + lax.erf(gate * (1.0 / math.sqrt(2.0))))
        bell = jnp.exp(-0.5 * gate * gate) * (1.0 / math.sqrt(2.0 * math.pi))
        curved = gate * share
        act_ref[at, :] = (curved * up).astype(LOW)
        grad_gate = (grad_act * up * (share + gate * bell)).astype(LOW)
        grad_up = (grad_act * curved).astype(LOW)
        dgate_ref[at, :] = grad_gate
        dup_ref[at, :] = grad_up
        part = dot(grad_gate, gate_w_ref[...]) + dot(grad_up, up_w_ref[...])
        part_ref[...] = part.astype(part_ref.dtype)
        more = jnp.sum(part * ref[...].astype(WIDE), 0, keepdims=True)
        gain_total = more if gain_total is None else gain_total + more
    gain_ref[...] = gain_total


def middle_back_kernel(
    mid_ref, grad_ref, keep_ref, core_ref, chip_ref, gain_ref, out_ref, low_ref
):
    total = keep_ref[...] + core_ref[...].astype(WIDE) + chip_ref[...].astype(WIDE)
    hat, scale = normalise(mid_ref[...])
    out = grad_ref[...].astype(WIDE) + normalise_back(total, hat, scale, gain_ref[...])
    out_ref[...] = out
    low_ref[...] = out.astype(LOW)


def hold_blocks(total, total_ref):
    blocks, rows, _ = total_ref.shape
    for block in range(blocks):
        total_ref[block] = total[block * rows : (block + 1) * rows]


def store_blocks(own_ref, kept_ref, away_ref, total_ref, bit, top, first):
    half_blocks, rows, _ = kept_ref.shape
    columns = slice(first, first + total_ref.shape[2])
    for index in range(half_blocks):
        place = (index >> bit << (bit + 1)) | (index & ((1 << bit) - 1))
        kept = total_ref[jnp.bitwise_xor(own_ref[0], place)]
        away = total_ref[jnp.bitwise_xor(own_ref[0], place | 1 << bit)]
        kept_ref[index, :, columns] = kept[top : top + rows]
        away_ref[index, :, columns] = away[top : top + rows].astype(LOW)


def wide_grad_kernel(own_ref, *refs, bits):
    count = 14
    kept_a, away_a, kept_b, away_b = refs[count : count + 4]
    total_ref = refs[count + 4]
    held = refs[count + 5 : 2 * count + 5]
    semaphores = refs[2 * count + 5]
    copies = [
        pltpu.make_async_copy(refs[index], held[index], semaphores.at[index])
        for index in range(count)
    ]
    for copy in copies:
        copy.start()
    rows = held[6].shape[0]
    units = held[0].shape[1]
    sums = [None, None, None]
    for place in range(4):
        if place % 2 == 0:
            for copy in copies[3 * (place // 2) : 3 * (place // 2) + 3]:
                copy.wait()
        for copy in copies[6 + 2 * place : 8 + 2 * place]:
            copy.wait()
        at = slice(place % 2 * rows, (place % 2 + 1) * rows)
        turned = held[6 + 2 * place][...].T
        turned_grad = held[7 + 2 * place][...].T
        for index, left in enumerate((turned, turned, turned_grad)):
            more = dot(left, held[3 * (place // 2) + index][at, :])
            sums[index] = more if sums[index] is None else sums[index] + more
    half_rows = kept_a.shape[1]
    for index in range(3):
        hold_blocks(sums[index], total_ref)
        store_blocks(own_ref, kept_a, away_a, total_ref, bits[0], 0, index * units)
        store_blocks(own_ref, kept_b, away_b, total_ref, bits[1], half_rows, index * units)


def attend_back_kernel(
    near_ref, far_ref, out_ref, total_ref, m0, m1, m2, m3, proj_ref, seg_row_ref, seg_col_ref,
    cos_ref, sin_ref, turned_ref, rows_near_ref, rows_far_ref,
    mixed_ref, keep_near_ref, keep_far_ref, away_near_ref, away_far_ref, gain_ref,
    keys_ref, values_ref, grad_ref, grad_keys_ref, grad_values_ref,
):
    length = seg_row_ref.shape[1]
    half_length = near_ref.shape[1]
    rows = m0.shape[0]
    width = proj_ref.shape[0]
    heads = width // HD
    half = HD // 2
    scale = 1.0 / math.sqrt(HD)
    for place, ref in enumerate((m0, m1, m2, m3)):
        grads = dot(proj_ref[...], ref[...], 1, 1)
        grad_ref[:, place * rows : (place + 1) * rows] = grads.astype(LOW)

    def turn_back(total, first, at):
        cosine, sine = cos_ref[:, at], sin_ref[:, at]
        lower, upper = total[:half], total[half:]
        turned_lower = (lower * cosine + upper * sine).astype(LOW)
        turned_upper = (upper * cosine - lower * sine).astype(LOW)
        mixed_ref[pl.ds(first, half), at] = turned_lower
        mixed_ref[pl.ds(pl.multiple_of(first + half, half), half), at] = turned_upper

    def slab(head, first):
        return pl.ds(pl.multiple_of(first + head * HD, HD), HD)

    @pl.loop(0, heads)
    def _(head):
        here, keys_at, values_at = slab(head, 0), slab(head, width), slab(head, 2 * width)
        for place, ref in enumerate((near_ref, far_ref)):
            at = slice(place * half_length, (place + 1) * half_length)
            keys_ref[at, :] = ref[keys_at, :].T
            values_ref[at, :] = ref[values_at, :].T
        for tile in range(length // TILE):
            ref = near_ref if tile * TILE < half_length else far_ref
            first = (tile * TILE) % half_length
            at = slice(tile * TILE, (tile + 1) * TILE)
            column = jnp.concatenate([seg_col_ref[...]] * (TILE // seg_col_ref.shape[1]), 1)
            same = column == seg_row_ref[:, at]
            query = ref[here, first : first + TILE]
            grads = grad_ref[here, at]
            delta = jnp.sum(
                grads.astype(WIDE) * out_ref[here, at].astype(WIDE), 0, keepdims=True
            )
            scores = dot(keys_ref[...], query) - total_ref[head, :, at]
            probs = jnp.exp(jnp.where(same, scores, MASK_FLOOR))
            prob_grads = dot(values_ref[...], grads)
            score_grads = (probs * (prob_grads - delta)).astype(LOW)
            low = probs.astype(LOW)
            grad_query = dot(near_ref[keys_at, :], score_grads[:half_length])
            grad_query += dot(far_ref[keys_at, :], score_grads[half_length:])
            turn_back(grad_query * scale, pl.multiple_of(head * HD, HD), at)
            more_keys = dot(query, score_grads, 1, 1)
            more_values = dot(grads, low, 1, 1)
            if tile == 0:
                grad_keys_ref[...] = more_keys
                grad_values_ref[...] = more_values
            else:
                grad_keys_ref[...] += more_keys
                grad_values_ref[...] += more_values
        turn_back(
            grad_keys_ref[...], pl.multiple_of(width + head * HD, HD), slice(0, length)
        )
        mixed_ref[values_at, :] = grad_values_ref[...].astype(LOW)

    refs = (keep_near_ref, away_near_ref, keep_far_ref, away_far_ref)
    for place, ref in enumerate(refs):
        part = dot(mixed_ref[:, place * rows : (place + 1) * rows], turned_ref[...], 0, 0)
        ref[...] = part.astype(ref.dtype)
        normed = (rows_near_ref, rows_far_ref)[place // 2][
            place % 2 * rows : (place % 2 + 1) * rows, :
        ]
        more = jnp.sum(part * normed.astype(WIDE), 0, keepdims=True)
        gain_total = more if place == 0 else gain_total + more
    gain_ref[...] = gain_total


def qkv_grad_kernel(
    own_ref, normed_a, normed_b, mixed_ref, m0, m1, m2, m3, attn_ref,
    kept_a, away_a, kept_b, away_b, total_ref, *, bits,
):
    rows = m0.shape[0]
    half_length = normed_a.shape[1]
    local = attn_ref.shape[0]
    total = dot(normed_a[...], mixed_ref[:, :half_length], 1, 1)
    total += dot(normed_b[...], mixed_ref[:, half_length:], 1, 1)
    hold_blocks(total[:, : 2 * local], total_ref)
    store_blocks(own_ref, kept_a, away_a, total_ref, bits[0], 0, 0)
    proj = None
    for place, ref in enumerate((m0, m1, m2, m3)):
        more = dot(ref[...].T, attn_ref[:, place * rows : (place + 1) * rows], 1, 1)
        proj = more if proj is None else proj + more
    hold_blocks(jnp.concatenate([total[:, 2 * local :], proj], 1), total_ref)
    store_blocks(own_ref, kept_b, away_b, total_ref, bits[1], 0, 0)


def finish_qkv_kernel(kept_a, came_a, kept_b, came_b, qkv_ref, proj_ref):
    local = proj_ref.shape[0]
    first = kept_a[...] + came_a[...].astype(WIDE)
    second = kept_b[...] + came_b[...].astype(WIDE)
    qkv_ref[0] = first[:, :local]
    qkv_ref[1] = first[:, local:]
    qkv_ref[2] = second[:, :local]
    proj_ref[...] = second[:, local:].T


def finish_wide_kernel(kept_a, came_a, kept_b, came_b, wide_ref, down_ref):
    units = down_ref.shape[0]
    half_rows = kept_a.shape[0]
    for place, (kept, came) in enumerate(((kept_a, came_a), (kept_b, came_b))):
        at = slice(place * half_rows, (place + 1) * half_rows)
        total = kept[...] + came[...].astype(WIDE)
        wide_ref[0, at, :] = total[:, :units]
        wide_ref[1, at, :] = total[:, units : 2 * units]
        down_ref[:, at] = total[:, 2 * units :].T


def last_kernel(x_ref, mid_ref, keep_ref, core_ref, chip_ref, gain_ref, out_ref):
    total = keep_ref[...] + core_ref[...].astype(WIDE) + chip_ref[...].astype(WIDE)
    hat, scale = normalise(x_ref[...].astype(WIDE))
    out_ref[...] = mid_ref[...] + normalise_back(total, hat, scale, gain_ref[...])


def output_kernel(act_a, act_b, down_ref, keep_near_ref, keep_far_ref, away_near_ref, away_far_ref):
    rows = keep_near_ref.shape[0]
    refs = (keep_near_ref, away_near_ref, keep_far_ref, away_far_ref)
    for place, ref in enumerate(refs):
        act = (act_a, act_b)[place // 2][place % 2 * rows : (place % 2 + 1) * rows, :]
        ref[...] = dot(act, down_ref[...]).astype(ref.dtype)


def reduce_parts(keep_far, away_far, away_near):
    came = swap(away_far, "tensor", 0)
    from_chip = swap((keep_far + came.astype(WIDE)).astype(LOW), "tensor", 1)
    return from_chip, swap(away_near, "tensor", 0)


def per_device(
    block_input,
    output_grad,
    segment_ids,
    positions,
    gain_one,
    gain_two,
    qkv_weight,
    proj_weight,
    wide_weight,
    down_weight,
):
    length = segment_ids.shape[1]
    rows, width = block_input.shape
    local = proj_weight.shape[0]
    heads = local // HD
    units = down_weight.shape[0]
    near = 2 * rows
    blocks = lax.axis_size("dp")
    own = lax.axis_index("dp").reshape(1)
    gain_a = gain_one.reshape(1, width)
    gain_b = gain_two.reshape(1, width)

    x_far = swap(block_input, "tensor", 1)
    x_core = swap(block_input, "tensor", 0)
    tables = ((HD // 2, length), WIDE)
    seg_row, seg_col, cosine, sine = call(
        functools.partial(prepare_kernel, count=lax.axis_size("tensor")),
        [((1, length), jnp.int32), ((length, 128), jnp.int32), tables, tables],
        lax.axis_index("tensor").reshape(1), segment_ids, positions,
        scalars=1,
    )
    turned = qkv_weight.reshape(width, 3 * local).T
    gate_w, up_w = wide_weight[:, 0].T, wide_weight[:, 1].T

    qkv_outs = [((width, near), LOW), ((near, width), LOW), ((3 * local, near), LOW)]
    qkv_flops = 2 * near * width * 3 * local
    normed_near, rows_near, mixed_near = call(
        functools.partial(qkv_kernel, offset=0), qkv_outs, block_input, x_core, gain_a, turned,
        cosine, sine, flops=qkv_flops,
    )
    x_both = swap(x_far, "tensor", 0)
    normed_far, rows_far, mixed_far = call(
        functools.partial(qkv_kernel, offset=near), qkv_outs, x_far, x_both, gain_a, turned,
        cosine, sine, flops=qkv_flops,
    )
    late, _ = lax.optimization_barrier((output_grad, x_far))
    g_far = swap(late, "tensor", 1)
    g_core = swap(late, "tensor", 0)
    g_both = swap(g_far, "tensor", 0)

    rows_wide, rows_low = ((rows, width), WIDE), ((rows, width), LOW)
    parts_outs = [rows_wide, rows_wide, rows_low, rows_low]
    attn, totals, keep_near, keep_far, away_near, away_far = call(
        attend_kernel,
        [((local, length), LOW), ((heads, 1, length), WIDE)] + parts_outs,
        mixed_near, mixed_far, seg_row, seg_col, proj_weight,
        scratch=[((heads, length, HD), LOW), ((local, length), LOW)],
        flops=16 * heads * length * length * HD,
    )
    from_chip, from_core = reduce_parts(keep_far, away_far, away_near)
    mid, n0 = call(
        middle_kernel, [rows_wide, rows_low],
        block_input, keep_near, from_core, from_chip, gain_b,
    )
    n2 = swap(n0, "tensor", 1)
    n1 = swap(n0, "tensor", 0)
    gain_row = ((1, width), WIDE)
    ff_outs = [((near, units), LOW)] * 3 + [rows_wide, rows_low, gain_row]
    ff_flops = 2 * near * width * units * 6
    dgate_near, dup_near, act_near, keep_near, away_near, gain_near = call(
        forward_kernel, ff_outs, n0, n1, output_grad, g_core, gate_w, up_w, down_weight,
        flops=ff_flops,
    )
    n3 = swap(n2, "tensor", 0)
    dgate_far, dup_far, act_far, keep_far, away_far, gain_far = call(
        forward_kernel, ff_outs, n2, n3, g_far, g_both, gate_w, up_w, down_weight,
        flops=ff_flops,
    )
    from_chip, from_core = reduce_parts(keep_far, away_far, away_near)
    grad_mid, m0 = call(
        middle_back_kernel, [rows_wide, rows_low],
        mid, output_grad, keep_near, from_core, from_chip, gain_b,
    )
    m2 = swap(m0, "tensor", 1)
    m1 = swap(m0, "tensor", 0)
    m3 = swap(m2, "tensor", 0)

    order = list(bits_of("dp"))
    turned_order = order[1:] + order[:1]
    firsts = (order[0], turned_order[0])
    half_rows = width // blocks // 2
    pieces = (blocks // 2, half_rows, 3 * units)
    kept_a, away_a, kept_b, away_b = call(
        functools.partial(wide_grad_kernel, bits=firsts),
        [(pieces, WIDE), (pieces, LOW), (pieces, WIDE), (pieces, LOW)],
        own, dgate_near, dup_near, act_near, dgate_far, dup_far, act_far,
        n0, output_grad, n1, g_core, n2, g_far, n3, g_both, streamed=True, limit=56,
        scratch=[((blocks, width // blocks, units), WIDE)],
        scalars=1, flops=2 * length * width * units * 3,
    )
    first = scatter_rows(kept_a, away_a, order)
    second = scatter_rows(kept_b, away_b, turned_order)
    grad_wide, grad_down = call(
        finish_wide_kernel,
        [((2, width // blocks, units), WIDE), ((units, width // blocks), WIDE)],
        *first, *second,
    )

    out_near, out_far, out_away_near, out_away_far = call(
        output_kernel, parts_outs, act_near, act_far, down_weight,
        flops=2 * length * width * units,
    )
    out_chip, out_core = reduce_parts(out_far, out_away_far, out_away_near)
    block_output = (
        mid + out_near + out_core.astype(WIDE) + out_chip.astype(WIDE)
    ).astype(LOW)

    grad_mixed, keep_near, keep_far, away_near, away_far, gain_part_one = call(
        attend_back_kernel,
        [((3 * local, length), LOW)] + parts_outs + [gain_row],
        mixed_near, mixed_far, attn, totals, m0, m1, m2, m3, proj_weight, seg_row, seg_col,
        cosine, sine, turned, rows_near, rows_far,
        scratch=[((length, HD), LOW), ((length, HD), LOW), ((local, length), LOW),
                 ((HD, length), WIDE), ((HD, length), WIDE)],
        flops=40 * heads * length * length * HD,
    )
    from_chip, from_core = reduce_parts(keep_far, away_far, away_near)
    pieces = (blocks // 2, width // blocks, 2 * local)
    kept_a, away_a, kept_b, away_b = call(
        functools.partial(qkv_grad_kernel, bits=firsts),
        [(pieces, WIDE), (pieces, LOW), (pieces, WIDE), (pieces, LOW)],
        own, normed_near, normed_far, grad_mixed, m0, m1, m2, m3, attn,
        scalars=1, flops=2 * length * width * local * 4,
        scratch=[((blocks, width // blocks, 2 * local), WIDE)],
    )
    first = scatter_rows(kept_a, away_a, order)
    second = scatter_rows(kept_b, away_b, turned_order)
    grad_qkv, grad_proj = call(
        finish_qkv_kernel,
        [((3, width // blocks, local), WIDE), ((local, width // blocks), WIDE)],
        *first, *second,
    )
    grad_gains = sum_everywhere(
        jnp.concatenate([gain_part_one / gain_a, (gain_near + gain_far) / gain_b], 0)
    )
    (grad_input,) = call(
        last_kernel, [rows_wide],
        block_input, grad_mid, keep_near, from_core, from_chip, gain_a,
    )
    return (
        block_output,
        grad_input,
        jnp.transpose(grad_qkv, (1, 0, 2)),
        grad_proj,
        jnp.transpose(grad_wide, (1, 0, 2)),
        grad_down,
        grad_gains,
    )


def solution(mesh):
    placed = (
        P(("dp", "tensor"), None),
        P(("dp", "tensor"), None),
        P("dp", None),
        P("dp", None),
        P(),
        P(),
        P(None, None, "tensor"),
        P("tensor", None),
        P(None, None, "tensor"),
        P("tensor", None),
    )
    return jax.shard_map(
        per_device,
        mesh=mesh,
        in_specs=placed,
        out_specs=(
            P(("dp", "tensor"), None),
            P(("dp", "tensor"), None),
            P("dp", None, "tensor"),
            P("tensor", "dp"),
            P("dp", None, "tensor"),
            P("tensor", "dp"),
            P(),
        ),
        check_vma=False,
    )
```

profile of v0, /device:TPU:0, one launch (start us, length us, event | category | flops | bytes accessed | tf_op | source)
XLA Modules:
  0.0 175.8 jit_solution(1906095852052916170)
XLA Ops:
  0.6 3.0 %collective-permute-start.1 = (bf16[256,768]{1,0:T(8,128)(2,1)}, bf16[256,768]{1,0:T(8,128)(2,1)S(1)}, u32[]{:S(2)}, u32[]{:S(2)}) collective-permute-start(bf16[256,768]{1,0:T(8,128)(2,1)} %x_ref.3), channel_id=1, source_target_pairs={{0,2},{1,3},{2,0},{3,1},{4,6},{5,7},{6,4},{7,5},{8,10},{9,11},{10,... | collective-permute-start | bytes 1179656 | tf_op jit(solution)/shard_map/ppermute | solution.py:29
  3.7 9.3 %collective-permute-done.1.near_ref = bf16[256,768]{1,0:T(8,128)(2,1)S(1)} collective-permute-done((bf16[256,768]{1,0:T(8,128)(2,1)}, bf16[256,768]{1,0:T(8,128)(2,1)S(1)}, u32[]{:S(2)}, u32[]{:S(2)}) %collective-permute-start.1) | collective-permute-done | bytes 393248 | tf_op jit(solution)/shard_map/ppermute | solution.py:29
  21.9 8.9 %shard_map.156 = (bf16[192,1024]{1,0:T(8,128)(2,1)S(1)}, f32[3,1,1024]{2,1,0:T(1,128)S(1)}, f32[256,768]{1,0:T(8,128)S(1)}, f32[256,768]{1,0:T(8,128)S(1)}, bf16...) custom-call(bf16[576,512]{1,0:T(8,128)(2,1)S(1)} %get-tuple-element.64.near_ref, ...), custom_call_target="tpu_custom_call" | custom-call | flops 3221225472 | bytes 2002944 | tf_op jit(solution)/shard_map/pallas_call | solution.py:66
  32.9 1.8 %collective-permute-start.5 = (bf16[256,768]{1,0:T(8,128)(2,1)S(1)}, bf16[256,768]{1,0:T(8,128)(2,1)S(1)}, u32[]{:S(2)}, u32[]{:S(2)}) collective-permute-start(bf16[256,768]{1,0:T(8,128)(2,1)S(1)} %add_convert_fusion.4), channel_id=1, source_target_pairs={{0,2},{1,3},{2,0},{3,1},{4,6},{5,7},{6,4},{7,5},{8,10},{9,11},{10,... | collective-permute-start | bytes 1179656 | tf_op jit(solution)/shard_map/ppermute | solution.py:29
  35.1 9.9 %collective-permute-done.5.chip_ref = bf16[256,768]{1,0:T(8,128)(2,1)S(1)} collective-permute-done((bf16[256,768]{1,0:T(8,128)(2,1)S(1)}, bf16[256,768]{1,0:T(8,128)(2,1)S(1)}, u32[]{:S(2)}, u32[]{:S(2)}) %collective-permute-start.5) | collective-permute-done | bytes 393248 | tf_op jit(solution)/shard_map/ppermute | solution.py:29
  48.4 5.1 %collective-permute-done.10.grad_near_ref.refs_11_ = bf16[256,768]{1,0:T(8,128)(2,1)} collective-permute-done((bf16[256,768]{1,0:T(8,128)(2,1)S(1)}, bf16[256,768]{1,0:T(8,128)(2,1)}, u32[]{:S(2)}, u32[]{:S(2)}) %collective-permute-start.10) | collective-permute-done | bytes 393248 | tf_op jit(solution)/shard_map/ppermute | solution.py:29
  53.5 7.8 %collective-permute-done.8.near_ref.refs_10_ = bf16[256,768]{1,0:T(8,128)(2,1)} collective-permute-done((bf16[256,768]{1,0:T(8,128)(2,1)}, bf16[256,768]{1,0:T(8,128)(2,1)}, u32[]{:S(2)}, u32[]{:S(2)}) %collective-permute-start.8) | collective-permute-done | bytes 393248 | tf_op jit(solution)/shard_map/ppermute | solution.py:29
  62.6 4.0 %shard_map.158 = (bf16[512,288]{1,0:T(8,128)(2,1)S(1)}, bf16[512,288]{1,0:T(8,128)(2,1)S(1)}, bf16[512,288]{1,0:T(8,128)(2,1)S(1)}, f32[256,768]{1,0:T(8,128)S(1...) custom-call(bf16[256,768]{1,0:T(8,128)(2,1)} %get-tuple-element.73.near_ref.refs_6_, ...), custom_call_target="tpu_custom_call" | custom-call | flops 1358954496 | bytes 2899968 | tf_op jit(solution)/shard_map/pallas_call | solution.py:66
  68.9 4.6 %shard_map.159 = (bf16[512,288]{1,0:T(8,128)(2,1)S(1)}, bf16[512,288]{1,0:T(8,128)(2,1)S(1)}, bf16[512,288]{1,0:T(8,128)(2,1)S(1)}, f32[256,768]{1,0:T(8,128)S(1...) custom-call(bf16[256,768]{1,0:T(8,128)(2,1)} %collective-permute-done.8.near_ref.refs_10_, ...), custom_call_target="tpu_custom_call" | custom-call | flops 1358954496 | bytes 2899968 | tf_op jit(solution)/shard_map/pallas_call | solution.py:66
  75.8 7.2 %shard_map.166 = (f32[4,48,864]{2,1,0:T(8,128)}, bf16[4,48,864]{2,1,0:T(8,128)(2,1)}, f32[4,48,864]{2,1,0:T(8,128)}, bf16[4,48,864]{2,1,0:T(8,128)(2,1)}) custom-call(s32[1]{0:T(128)} %bitcast.10.own_ref, bf16[512,288]{1,0:T(8,128)(2,1)} %copy-done.14, bf16[512,288]{1,0:T(8,128)(2,1)} %copy-done.15, bf16[512,288]{1,0:T(8,128)(2,1)} %copy-done.10, ...), custom_call_target="tpu_custom_call" | custom-call | flops 1358954496 | bytes 4915204 | tf_op jit(solution)/shard_map/pallas_call | solution.py:66
  83.0 1.8 %collective-permute-start.30 = (bf16[4,48,864]{2,1,0:T(8,128)(2,1)}, bf16[4,48,864]{2,1,0:T(8,128)(2,1)S(1)}, u32[]{:S(2)}, u32[]{:S(2)}) collective-permute-start(bf16[4,48,864]{2,1,0:T(8,128)(2,1)} %get-tuple-element.109), channel_id=1, source_target_pairs={{0,4},{4,0},{8,12},{12,8},{16,20},{20,16},{24,28},{28,24},{1,5},{5... | collective-permute-start | bytes 995336 | tf_op jit(solution)/shard_map/ppermute | solution.py:29
  88.2 5.6 %collective-permute-done.30 = bf16[4,48,864]{2,1,0:T(8,128)(2,1)S(1)} collective-permute-done((bf16[4,48,864]{2,1,0:T(8,128)(2,1)}, bf16[4,48,864]{2,1,0:T(8,128)(2,1)S(1)}, u32[]{:S(2)}, u32[]{:S(2)}) %collective-permute-start.30) | collective-permute-done | bytes 331808 | tf_op jit(solution)/shard_map/ppermute | solution.py:29
  93.9 1.8 %collective-permute-start.17 = (bf16[256,768]{1,0:T(8,128)(2,1)S(1)}, bf16[256,768]{1,0:T(8,128)(2,1)S(1)}, u32[]{:S(2)}, u32[]{:S(2)}) collective-permute-start(bf16[256,768]{1,0:T(8,128)(2,1)S(1)} %add_convert_fusion.1), channel_id=1, source_target_pairs={{0,2},{1,3},{2,0},{3,1},{4,6},{5,7},{6,4},{7,5},{8,10},{9,11},{10,... | collective-permute-start | bytes 1179656 | tf_op jit(solution)/shard_map/ppermute | solution.py:29
  97.5 2.7 %collective-permute-start.34 = (bf16[2,48,864]{2,1,0:T(8,128)(2,1)S(1)}, bf16[2,48,864]{2,1,0:T(8,128)(2,1)S(1)}, u32[]{:S(2)}, u32[]{:S(2)}) collective-permute-start(bf16[2,48,864]{2,1,0:T(8,128)(2,1)S(1)} %slice.122), channel_id=1, source_target_pairs={{0,16},{4,20},{8,24},{12,28},{16,0},{20,4},{24,8},{28,12},{1,17},{... | collective-permute-start | bytes 497672 | tf_op jit(solution)/shard_map/ppermute | solution.py:29
  100.1 5.4 %collective-permute-done.17.chip_ref = bf16[256,768]{1,0:T(8,128)(2,1)S(1)} collective-permute-done((bf16[256,768]{1,0:T(8,128)(2,1)S(1)}, bf16[256,768]{1,0:T(8,128)(2,1)S(1)}, u32[]{:S(2)}, u32[]{:S(2)}) %collective-permute-start.17) | collective-permute-done | bytes 393248 | tf_op jit(solution)/shard_map/ppermute | solution.py:29
  108.5 9.6 %collective-permute-done.19.m2 = bf16[256,768]{1,0:T(8,128)(2,1)S(1)} collective-permute-done((bf16[256,768]{1,0:T(8,128)(2,1)S(1)}, bf16[256,768]{1,0:T(8,128)(2,1)S(1)}, u32[]{:S(2)}, u32[]{:S(2)}) %collective-permute-start.19) | collective-permute-done | bytes 393248 | tf_op jit(solution)/shard_map/ppermute | solution.py:29
  118.2 2.9 %collective-permute-start.32 = (bf16[48,864]{1,0:T(8,128)(2,1)S(1)}, bf16[48,864]{1,0:T(8,128)(2,1)S(1)}, u32[]{:S(2)}, u32[]{:S(2)}) collective-permute-start(bf16[48,864]{1,0:T(8,128)(2,1)S(1)} %fusion.4), channel_id=1, source_target_pairs={{0,16},{4,20},{8,24},{12,28},{16,0},{20,4},{24,8},{28,12},{1,17},{... | collective-permute-start | bytes 248840 | tf_op jit(solution)/shard_map/ppermute | solution.py:29
  121.2 12.6 %shard_map.162 = (bf16[576,1024]{1,0:T(8,128)(2,1)S(1)}, f32[256,768]{1,0:T(8,128)S(1)}, f32[256,768]{1,0:T(8,128)S(1)}, bf16[256,768]{1,0:T(8,128)(2,1)S(1)}, b...) custom-call(bf16[576,512]{1,0:T(8,128)(2,1)S(1)} %copy-done.25, bf16[576,512]{1,0:T(8,128)(2,1)S(1)} %copy-done.27, ...), custom_call_target="tpu_custom_call" | custom-call | flops 8053063680 | bytes 6701056 | tf_op jit(solution)/shard_map/pallas_call | solution.py:66
  135.5 2.1 %collective-permute-done.36 = f32[2,768]{1,0:T(2,128)S(1)} collective-permute-done((f32[2,768]{1,0:T(2,128)S(1)}, f32[2,768]{1,0:T(2,128)S(1)}, u32[]{:S(2)}, u32[]{:S(2)}) %collective-permute-start.36) | collective-permute-done | bytes 6176 | tf_op jit(solution)/shard_map/ppermute | solution.py:29
  141.0 2.1 %shard_map.164 = (f32[4,96,384]{2,1,0:T(8,128)S(1)}, bf16[4,96,384]{2,1,0:T(8,128)(2,1)S(1)}, f32[4,96,384]{2,1,0:T(8,128)S(1)}, bf16[4,96,384]{2,1,0:T(8,128)(2,1)S(1)}) custom-call(s32[1]{0:T(128)} %bitcast.10.own_ref, bf16[768,512]{1,0:T(8,128)(2,1)S(1)} %get-tuple-element.95.normed_a, bf16[768,512]{1,0:T(8,128)(2,1)S(1)} %copy-done.7, ...), custom_call_target="tpu_custom_call" | custom-call | flops 1207959552 | bytes 4718596 | tf_op jit(solution)/shard_map/pallas_call | solution.py:66
  154.7 6.8 %collective-permute-done.27 = bf16[4,96,384]{2,1,0:T(8,128)(2,1)S(1)} collective-permute-done((bf16[4,96,384]{2,1,0:T(8,128)(2,1)S(1)}, bf16[4,96,384]{2,1,0:T(8,128)(2,1)S(1)}, u32[]{:S(2)}, u32[]{:S(2)}) %collective-permute-start.27) | collective-permute-done | bytes 294944 | tf_op jit(solution)/shard_map/ppermute | solution.py:29
  163.1 2.2 %collective-permute-start.26 = (bf16[96,384]{1,0:T(8,128)(2,1)S(1)}, bf16[96,384]{1,0:T(8,128)(2,1)S(1)}, u32[]{:S(2)}, u32[]{:S(2)}) collective-permute-start(bf16[96,384]{1,0:T(8,128)(2,1)S(1)} %fusion.6), channel_id=1, source_target_pairs={{0,16},{4,20},{8,24},{12,28},{16,0},{20,4},{24,8},{28,12},{1,17},{... | collective-permute-start | bytes 221192 | tf_op jit(solution)/shard_map/ppermute | solution.py:29
  165.3 3.6 %collective-permute-done.28 = bf16[2,96,384]{2,1,0:T(8,128)(2,1)S(1)} collective-permute-done((bf16[2,96,384]{2,1,0:T(8,128)(2,1)S(1)}, bf16[2,96,384]{2,1,0:T(8,128)(2,1)S(1)}, u32[]{:S(2)}, u32[]{:S(2)}) %collective-permute-start.28) | collective-permute-done | bytes 147488 | tf_op jit(solution)/shard_map/ppermute | solution.py:29
  170.5 2.9 %collective-permute-done.29.came_b = bf16[96,384]{1,0:T(8,128)(2,1)S(1)} collective-permute-done((bf16[96,384]{1,0:T(8,128)(2,1)S(1)}, bf16[96,384]{1,0:T(8,128)(2,1)S(1)}, u32[]{:S(2)}, u32[]{:S(2)}) %collective-permute-start.29) | collective-permute-done | bytes 73760 | tf_op jit(solution)/shard_map/ppermute | solution.py:29
  (184 shorter events, 50.8 us)
Async XLA Ops:
  0.6 12.4 %collective-permute-start.1 = (bf16[256,768]{1,0:T(8,128)(2,1)}, bf16[256,768]{1,0:T(8,128)(2,1)S(1)}, u32[]{:S(2)}, u32[]{:S(2)}) collective-permute-start(bf16[256,768]{1,0:T(8,128)(2,1)} %x_ref.3), channel_id=1, source_target_pairs={{0,2},{1,3},{2,0},{3,1},{4,6},{5,7},{6,4},{7,5},{8,10},{9,11},{10,... | collective-permute-start | bytes 1179656 | tf_op jit(solution)/shard_map/ppermute | solution.py:29
  3.7 11.9 %collective-permute-start = (bf16[256,768]{1,0:T(8,128)(2,1)}, bf16[256,768]{1,0:T(8,128)(2,1)S(1)}, u32[]{:S(2)}, u32[]{:S(2)}) collective-permute-start(bf16[256,768]{1,0:T(8,128)(2,1)} %x_ref.3), channel_id=1, source_target_pairs={{0,1},{1,0},{2,3},{3,2},{4,5},{5,4},{6,7},{7,6},{8,9},{9,8},{10,11... | collective-permute-start | bytes 1179656 | tf_op jit(solution)/shard_map/ppermute | solution.py:29
  32.9 12.1 %collective-permute-start.5 = (bf16[256,768]{1,0:T(8,128)(2,1)S(1)}, bf16[256,768]{1,0:T(8,128)(2,1)S(1)}, u32[]{:S(2)}, u32[]{:S(2)}) collective-permute-start(bf16[256,768]{1,0:T(8,128)(2,1)S(1)} %add_convert_fusion.4), channel_id=1, source_target_pairs={{0,2},{1,3},{2,0},{3,1},{4,6},{5,7},{6,4},{7,5},{8,10},{9,11},{10,... | collective-permute-start | bytes 1179656 | tf_op jit(solution)/shard_map/ppermute | solution.py:29
  34.7 18.8 %collective-permute-start.10 = (bf16[256,768]{1,0:T(8,128)(2,1)S(1)}, bf16[256,768]{1,0:T(8,128)(2,1)}, u32[]{:S(2)}, u32[]{:S(2)}) collective-permute-start(bf16[256,768]{1,0:T(8,128)(2,1)S(1)} %copy-done.4), channel_id=1, source_target_pairs={{0,2},{1,3},{2,0},{3,1},{4,6},{5,7},{6,4},{7,5},{8,10},{9,11},{10,... | collective-permute-start | bytes 1179656 | tf_op jit(solution)/shard_map/ppermute | solution.py:29
  46.1 15.2 %collective-permute-start.8 = (bf16[256,768]{1,0:T(8,128)(2,1)}, bf16[256,768]{1,0:T(8,128)(2,1)}, u32[]{:S(2)}, u32[]{:S(2)}) collective-permute-start(bf16[256,768]{1,0:T(8,128)(2,1)} %get-tuple-element.73.near_ref.refs_6_), channel_id=1, source_target_pairs={{0,2},{1,3},{2,0},{3,1},{4,6},{5,7},{6,4},{7,5},{8,10},{9,11},{10,... | collective-permute-start | bytes 1179656 | tf_op jit(solution)/shard_map/ppermute | solution.py:29
  47.9 14.8 %collective-permute-start.7 = (bf16[256,768]{1,0:T(8,128)(2,1)S(1)}, bf16[256,768]{1,0:T(8,128)(2,1)}, u32[]{:S(2)}, u32[]{:S(2)}) collective-permute-start(bf16[256,768]{1,0:T(8,128)(2,1)S(1)} %copy-done.4), channel_id=1, source_target_pairs={{0,1},{1,0},{2,3},{3,2},{4,5},{5,4},{6,7},{7,6},{8,9},{9,8},{10,11... | collective-permute-start | bytes 1179656 | tf_op jit(solution)/shard_map/ppermute | solution.py:29
  47.9 14.8 %collective-permute-start.6 = (bf16[256,768]{1,0:T(8,128)(2,1)}, bf16[256,768]{1,0:T(8,128)(2,1)}, u32[]{:S(2)}, u32[]{:S(2)}) collective-permute-start(bf16[256,768]{1,0:T(8,128)(2,1)} %get-tuple-element.73.near_ref.refs_6_), channel_id=1, source_target_pairs={{0,1},{1,0},{2,3},{3,2},{4,5},{5,4},{6,7},{7,6},{8,9},{9,8},{10,11... | collective-permute-start | bytes 1179656 | tf_op jit(solution)/shard_map/ppermute | solution.py:29
  53.5 15.4 %collective-permute-start.11 = (bf16[256,768]{1,0:T(8,128)(2,1)}, bf16[256,768]{1,0:T(8,128)(2,1)}, u32[]{:S(2)}, u32[]{:S(2)}) collective-permute-start(bf16[256,768]{1,0:T(8,128)(2,1)} %collective-permute-done.10.grad_near_ref.refs_11_), channel_id=1, source_target_pairs={{0,1},{1,0},{2,3},{3,2},{4,5},{5,4},{6,7},{7,6},{8,9},{9,8},{10,11... | collective-permute-start | bytes 1179656 | tf_op jit(solution)/shard_map/ppermute | solution.py:29
  83.0 10.8 %collective-permute-start.30 = (bf16[4,48,864]{2,1,0:T(8,128)(2,1)}, bf16[4,48,864]{2,1,0:T(8,128)(2,1)S(1)}, u32[]{:S(2)}, u32[]{:S(2)}) collective-permute-start(bf16[4,48,864]{2,1,0:T(8,128)(2,1)} %get-tuple-element.109), channel_id=1, source_target_pairs={{0,4},{4,0},{8,12},{12,8},{16,20},{20,16},{24,28},{28,24},{1,5},{5... | collective-permute-start | bytes 995336 | tf_op jit(solution)/shard_map/ppermute | solution.py:29
  84.8 12.7 %collective-permute-start.15 = (bf16[256,768]{1,0:T(8,128)(2,1)S(1)}, bf16[256,768]{1,0:T(8,128)(2,1)S(1)}, u32[]{:S(2)}, u32[]{:S(2)}) collective-permute-start(bf16[256,768]{1,0:T(8,128)(2,1)S(1)} %get-tuple-element.82), channel_id=1, source_target_pairs={{0,1},{1,0},{2,3},{3,2},{4,5},{5,4},{6,7},{7,6},{8,9},{9,8},{10,11... | collective-permute-start | bytes 1179656 | tf_op jit(solution)/shard_map/ppermute | solution.py:29
  85.0 10.7 %collective-permute-start.33 = (bf16[4,48,864]{2,1,0:T(8,128)(2,1)}, bf16[4,48,864]{2,1,0:T(8,128)(2,1)S(1)}, u32[]{:S(2)}, u32[]{:S(2)}) collective-permute-start(bf16[4,48,864]{2,1,0:T(8,128)(2,1)} %get-tuple-element.111), channel_id=1, source_target_pairs={{0,8},{4,12},{8,0},{12,4},{16,24},{20,28},{24,16},{28,20},{1,9},{5... | collective-permute-start | bytes 995336 | tf_op jit(solution)/shard_map/ppermute | solution.py:29
  87.6 62.7 %collective-permute-start.12 = (bf16[256,768]{1,0:T(8,128)(2,1)S(1)}, bf16[256,768]{1,0:T(8,128)(2,1)S(1)}, u32[]{:S(2)}, u32[]{:S(2)}) collective-permute-start(bf16[256,768]{1,0:T(8,128)(2,1)S(1)} %get-tuple-element.78), channel_id=1, source_target_pairs={{0,1},{1,0},{2,3},{3,2},{4,5},{5,4},{6,7},{7,6},{8,9},{9,8},{10,11... | collective-permute-start | bytes 1179656 | tf_op jit(solution)/shard_map/ppermute | solution.py:29
  93.7 14.2 %collective-permute-start.13 = (bf16[256,768]{1,0:T(8,128)(2,1)S(1)}, bf16[256,768]{1,0:T(8,128)(2,1)S(1)}, u32[]{:S(2)}, u32[]{:S(2)}) collective-permute-start(bf16[256,768]{1,0:T(8,128)(2,1)S(1)} %get-tuple-element.80), channel_id=1, source_target_pairs={{0,1},{1,0},{2,3},{3,2},{4,5},{5,4},{6,7},{7,6},{8,9},{9,8},{10,11... | collective-permute-start | bytes 1179656 | tf_op jit(solution)/shard_map/ppermute | solution.py:29
  93.9 11.6 %collective-permute-start.17 = (bf16[256,768]{1,0:T(8,128)(2,1)S(1)}, bf16[256,768]{1,0:T(8,128)(2,1)S(1)}, u32[]{:S(2)}, u32[]{:S(2)}) collective-permute-start(bf16[256,768]{1,0:T(8,128)(2,1)S(1)} %add_convert_fusion.1), channel_id=1, source_target_pairs={{0,2},{1,3},{2,0},{3,1},{4,6},{5,7},{6,4},{7,5},{8,10},{9,11},{10,... | collective-permute-start | bytes 1179656 | tf_op jit(solution)/shard_map/ppermute | solution.py:29
  95.7 12.7 %collective-permute-start.31 = (bf16[2,48,864]{2,1,0:T(8,128)(2,1)S(1)}, bf16[2,48,864]{2,1,0:T(8,128)(2,1)S(1)}, u32[]{:S(2)}, u32[]{:S(2)}) collective-permute-start(bf16[2,48,864]{2,1,0:T(8,128)(2,1)S(1)} %fusion.2), channel_id=1, source_target_pairs={{0,8},{4,12},{8,0},{12,4},{16,24},{20,28},{24,16},{28,20},{1,9},{5... | collective-permute-start | bytes 497672 | tf_op jit(solution)/shard_map/ppermute | solution.py:29
  97.5 20.7 %collective-permute-start.34 = (bf16[2,48,864]{2,1,0:T(8,128)(2,1)S(1)}, bf16[2,48,864]{2,1,0:T(8,128)(2,1)S(1)}, u32[]{:S(2)}, u32[]{:S(2)}) collective-permute-start(bf16[2,48,864]{2,1,0:T(8,128)(2,1)S(1)} %slice.122), channel_id=1, source_target_pairs={{0,16},{4,20},{8,24},{12,28},{16,0},{20,4},{24,8},{28,12},{1,17},{... | collective-permute-start | bytes 497672 | tf_op jit(solution)/shard_map/ppermute | solution.py:29
  106.1 12.1 %collective-permute-start.19 = (bf16[256,768]{1,0:T(8,128)(2,1)S(1)}, bf16[256,768]{1,0:T(8,128)(2,1)S(1)}, u32[]{:S(2)}, u32[]{:S(2)}) collective-permute-start(bf16[256,768]{1,0:T(8,128)(2,1)S(1)} %get-tuple-element.88.m0), channel_id=1, source_target_pairs={{0,2},{1,3},{2,0},{3,1},{4,6},{5,7},{6,4},{7,5},{8,10},{9,11},{10,... | collective-permute-start | bytes 1179656 | tf_op jit(solution)/shard_map/ppermute | solution.py:29
  108.0 42.3 %collective-permute-start.14 = (bf16[256,768]{1,0:T(8,128)(2,1)S(1)}, bf16[256,768]{1,0:T(8,128)(2,1)S(1)}, u32[]{:S(2)}, u32[]{:S(2)}) collective-permute-start(bf16[256,768]{1,0:T(8,128)(2,1)S(1)} %add_convert_fusion.3), channel_id=1, source_target_pairs={{0,2},{1,3},{2,0},{3,1},{4,6},{5,7},{6,4},{7,5},{8,10},{9,11},{10,... | collective-permute-start | bytes 1179656 | tf_op jit(solution)/shard_map/ppermute | solution.py:29
  108.5 12.7 %collective-permute-start.18 = (bf16[256,768]{1,0:T(8,128)(2,1)S(1)}, bf16[256,768]{1,0:T(8,128)(2,1)S(1)}, u32[]{:S(2)}, u32[]{:S(2)}) collective-permute-start(bf16[256,768]{1,0:T(8,128)(2,1)S(1)} %get-tuple-element.88.m0), channel_id=1, source_target_pairs={{0,1},{1,0},{2,3},{3,2},{4,5},{5,4},{6,7},{7,6},{8,9},{9,8},{10,11... | collective-permute-start | bytes 1179656 | tf_op jit(solution)/shard_map/ppermute | solution.py:29
  118.2 26.0 %collective-permute-start.32 = (bf16[48,864]{1,0:T(8,128)(2,1)S(1)}, bf16[48,864]{1,0:T(8,128)(2,1)S(1)}, u32[]{:S(2)}, u32[]{:S(2)}) collective-permute-start(bf16[48,864]{1,0:T(8,128)(2,1)S(1)} %fusion.4), channel_id=1, source_target_pairs={{0,16},{4,20},{8,24},{12,28},{16,0},{20,4},{24,8},{28,12},{1,17},{... | collective-permute-start | bytes 248840 | tf_op jit(solution)/shard_map/ppermute | solution.py:29
  143.1 10.8 %collective-permute-start.24 = (bf16[4,96,384]{2,1,0:T(8,128)(2,1)S(1)}, bf16[4,96,384]{2,1,0:T(8,128)(2,1)S(1)}, u32[]{:S(2)}, u32[]{:S(2)}) collective-permute-start(bf16[4,96,384]{2,1,0:T(8,128)(2,1)S(1)} %get-tuple-element.99), channel_id=1, source_target_pairs={{0,4},{4,0},{8,12},{12,8},{16,20},{20,16},{24,28},{28,24},{1,5},{5... | collective-permute-start | bytes 884744 | tf_op jit(solution)/shard_map/ppermute | solution.py:29
  151.2 10.2 %collective-permute-start.27 = (bf16[4,96,384]{2,1,0:T(8,128)(2,1)S(1)}, bf16[4,96,384]{2,1,0:T(8,128)(2,1)S(1)}, u32[]{:S(2)}, u32[]{:S(2)}) collective-permute-start(bf16[4,96,384]{2,1,0:T(8,128)(2,1)S(1)} %get-tuple-element.101), channel_id=1, source_target_pairs={{0,8},{4,12},{8,0},{12,4},{16,24},{20,28},{24,16},{28,20},{1,9},{5... | collective-permute-start | bytes 884744 | tf_op jit(solution)/shard_map/ppermute | solution.py:29
  152.7 21.6 %collective-permute-start.21 = (bf16[256,768]{1,0:T(8,128)(2,1)S(1)}, bf16[256,768]{1,0:T(8,128)(2,1)S(1)}, u32[]{:S(2)}, u32[]{:S(2)}) collective-permute-start(bf16[256,768]{1,0:T(8,128)(2,1)S(1)} %get-tuple-element.92), channel_id=1, source_target_pairs={{0,1},{1,0},{2,3},{3,2},{4,5},{5,4},{6,7},{7,6},{8,9},{9,8},{10,11... | collective-permute-start | bytes 1179656 | tf_op jit(solution)/shard_map/ppermute | solution.py:29
  161.9 12.4 %collective-permute-start.23 = (bf16[256,768]{1,0:T(8,128)(2,1)S(1)}, bf16[256,768]{1,0:T(8,128)(2,1)S(1)}, u32[]{:S(2)}, u32[]{:S(2)}) collective-permute-start(bf16[256,768]{1,0:T(8,128)(2,1)S(1)} %add_convert_fusion), channel_id=1, source_target_pairs={{0,2},{1,3},{2,0},{3,1},{4,6},{5,7},{6,4},{7,5},{8,10},{9,11},{10,... | collective-permute-start | bytes 1179656 | tf_op jit(solution)/shard_map/ppermute | solution.py:29
  (54 other events, 354.7 us)
where the time goes:
time: 176 us
  waiting for transfers between devices  71.5 us (41%)
  Pallas kernels  48.1 us (27%)
  starting transfers between devices  39.5 us (22%)
  local copies, waits for them, and re-layouts  13.2 us (8%)
  other arithmetic  2.24 us (1%)
    ppermute x41, waiting for transfers between devices, swap(): lax.ppermute(values_in, axis, [(i, i ^ 1 << bit) for i in range(size)])  71.5 us
    pallas_call x15, Pallas kernels, call(): pl.pallas_call(kernel, out_shape=shapes, in_specs=spaces, out_specs=[pl.B...  48.1 us
    ppermute x41, starting transfers between devices, swap(): lax.ppermute(values_in, axis, [(i, i ^ 1 << bit) for i in range(size)])  39.5 us
    unnamed x75, local copies, waits for them, and re-layouts  11 us
  transfers between devices with their start and end apart: 41, of which 15 were waited for; matrix products, arithmetic and copies ran while one was open for 3% of the time, Pallas kernels for 14%

commit v1 on v0

--- a/solution.py
+++ b/solution.py
@@ -24,15 +24,17 @@
     return range(int(math.log2(lax.axis_size(axis))))
 
 
+def exchange(values_in, axis, mask):
+    size = lax.axis_size(axis)
+    return lax.ppermute(values_in, axis, [(i, i ^ mask) for i in range(size)])
+
+
 def swap(values_in, axis, bit):
-    size = lax.axis_size(axis)
-    return lax.ppermute(values_in, axis, [(i, i ^ (1 << bit)) for i in range(size)])
+    return exchange(values_in, axis, 1 << bit)
 
 
 def sum_everywhere(values_in):
-    steps = [("dp", bit) for bit in bits_of("dp")]
-    steps[1:1] = [("tensor", 0)]
-    steps += [("tensor", bit) for bit in bits_of("tensor") if bit]
+    steps = [(axis, bit) for axis in ("tensor", "dp") for bit in bits_of(axis)]
     for axis, bit in steps:
         values_in = values_in + swap(values_in, axis, bit)
     return values_in
@@ -139,13 +141,13 @@
 
 
 def attend_kernel(
-    near_ref, far_ref, seg_row_ref, seg_col_ref, proj_ref,
-    out_ref, total_ref, keep_near_ref, keep_far_ref, away_near_ref, away_far_ref,
+    near_ref, far_ref, seg_row_ref, seg_col_ref,
+    out_ref, total_ref, part0_ref, part1_ref, part2_ref, part3_ref,
     keys_ref, values_ref,
 ):
     length = seg_row_ref.shape[1]
     half_length = near_ref.shape[1]
-    width = proj_ref.shape[0]
+    width = out_ref.shape[0]
     heads = width // HD
     for place, ref in enumerate((near_ref, far_ref)):
         at = slice(place * half_length, (place + 1) * half_length)
@@ -168,16 +170,15 @@
             mixed = dot(values_ref[head * HD : (head + 1) * HD, :], raised.astype(LOW))
             out_ref[head * HD : (head + 1) * HD, at] = (mixed / total).astype(LOW)
             total_ref[head, :, at] = top + jnp.log(total)
-    rows = keep_near_ref.shape[0]
-    refs = (keep_near_ref, away_near_ref, keep_far_ref, away_far_ref)
-    for place, ref in enumerate(refs):
-        part = dot(out_ref[:, place * rows : (place + 1) * rows], proj_ref[...], 0, 0)
-        ref[...] = part.astype(ref.dtype)
-
-
-def middle_kernel(x_ref, keep_ref, core_ref, chip_ref, gain_ref, mid_ref, normed_ref):
-    total = x_ref[...].astype(WIDE) + keep_ref[...]
-    total = total + core_ref[...].astype(WIDE) + chip_ref[...].astype(WIDE)
+    rows = part0_ref.shape[1]
+    for place, ref in enumerate((part0_ref, part1_ref, part2_ref, part3_ref)):
+        ref[...] = out_ref[:, place * rows : (place + 1) * rows]
+
+
+def middle_kernel(x_ref, a0, a1, a2, a3, w0, w1, w2, w3, gain_ref, mid_ref, normed_ref):
+    total = x_ref[...].astype(WIDE)
+    for attn, weight in ((a0, w0), (a1, w1), (a2, w2), (a3, w3)):
+        total = total + dot(attn[...], weight[...], 0, 0)
     mid_ref[...] = total
     normed_ref[...] = (normalise(total)[0] * gain_ref[...]).astype(LOW)
 
@@ -210,13 +211,26 @@
 
 
 def middle_back_kernel(
-    mid_ref, grad_ref, keep_ref, core_ref, chip_ref, gain_ref, out_ref, low_ref
+    mid_ref, grad_ref, keep_ref, core_ref, chip_ref, gain_ref, w0, w1, w2, w3,
+    out_ref, low_ref, part0_ref, part1_ref, part2_ref, part3_ref,
 ):
     total = keep_ref[...] + core_ref[...].astype(WIDE) + chip_ref[...].astype(WIDE)
     hat, scale = normalise(mid_ref[...])
     out = grad_ref[...].astype(WIDE) + normalise_back(total, hat, scale, gain_ref[...])
     out_ref[...] = out
-    low_ref[...] = out.astype(LOW)
+    low = out.astype(LOW)
+    low_ref[...] = low
+    parts = (part0_ref, part1_ref, part2_ref, part3_ref)
+    for weight, ref in zip((w0, w1, w2, w3), parts):
+        ref[...] = dot(weight[...], low, 1, 1).astype(LOW)
+
+
+def proj_grad_kernel(
+    a0, a1, a2, a3, grad_ref, keep_near_ref, keep_far_ref, away_near_ref, away_far_ref
+):
+    refs = (keep_near_ref, away_near_ref, keep_far_ref, away_far_ref)
+    for attn, ref in zip((a0, a1, a2, a3), refs):
+        ref[...] = dot(attn[...], grad_ref[...]).astype(ref.dtype)
 
 
 def hold_blocks(total, total_ref):
@@ -271,21 +285,20 @@
 
 
 def attend_back_kernel(
-    near_ref, far_ref, out_ref, total_ref, m0, m1, m2, m3, proj_ref, seg_row_ref, seg_col_ref,
+    near_ref, far_ref, out_ref, total_ref, g0, g1, g2, g3, seg_row_ref, seg_col_ref,
     cos_ref, sin_ref, turned_ref, rows_near_ref, rows_far_ref,
     mixed_ref, keep_near_ref, keep_far_ref, away_near_ref, away_far_ref, gain_ref,
     keys_ref, values_ref, grad_ref, grad_keys_ref, grad_values_ref,
 ):
     length = seg_row_ref.shape[1]
     half_length = near_ref.shape[1]
-    rows = m0.shape[0]
-    width = proj_ref.shape[0]
+    rows = g0.shape[1]
+    width = g0.shape[0]
     heads = width // HD
     half = HD // 2
     scale = 1.0 / math.sqrt(HD)
-    for place, ref in enumerate((m0, m1, m2, m3)):
-        grads = dot(proj_ref[...], ref[...], 1, 1)
-        grad_ref[:, place * rows : (place + 1) * rows] = grads.astype(LOW)
+    for place, ref in enumerate((g0, g1, g2, g3)):
+        grad_ref[:, place * rows : (place + 1) * rows] = ref[...]
 
     def turn_back(total, first, at):
         cosine, sine = cos_ref[:, at], sin_ref[:, at]
@@ -350,21 +363,17 @@
 
 
 def qkv_grad_kernel(
-    own_ref, normed_a, normed_b, mixed_ref, m0, m1, m2, m3, attn_ref,
+    own_ref, normed_a, normed_b, mixed_ref, proj_keep, proj_core, proj_chip,
     kept_a, away_a, kept_b, away_b, total_ref, *, bits,
 ):
-    rows = m0.shape[0]
     half_length = normed_a.shape[1]
-    local = attn_ref.shape[0]
+    local = proj_keep.shape[0]
     total = dot(normed_a[...], mixed_ref[:, :half_length], 1, 1)
     total += dot(normed_b[...], mixed_ref[:, half_length:], 1, 1)
     hold_blocks(total[:, : 2 * local], total_ref)
     store_blocks(own_ref, kept_a, away_a, total_ref, bits[0], 0, 0)
-    proj = None
-    for place, ref in enumerate((m0, m1, m2, m3)):
-        more = dot(ref[...].T, attn_ref[:, place * rows : (place + 1) * rows], 1, 1)
-        proj = more if proj is None else proj + more
-    hold_blocks(jnp.concatenate([total[:, 2 * local :], proj], 1), total_ref)
+    proj = proj_keep[...] + proj_core[...].astype(WIDE) + proj_chip[...].astype(WIDE)
+    hold_blocks(jnp.concatenate([total[:, 2 * local :], proj.T], 1), total_ref)
     store_blocks(own_ref, kept_b, away_b, total_ref, bits[1], 0, 0)
 
 
@@ -455,24 +464,30 @@
         functools.partial(qkv_kernel, offset=near), qkv_outs, x_far, x_both, gain_a, turned,
         cosine, sine, flops=qkv_flops,
     )
-    late, _ = lax.optimization_barrier((output_grad, x_far))
-    g_far = swap(late, "tensor", 1)
-    g_core = swap(late, "tensor", 0)
+    w0 = proj_weight
+    w2 = swap(w0, "tensor", 1)
+    w1 = swap(w0, "tensor", 0)
+    w3 = swap(w2, "tensor", 0)
+    g_far = swap(output_grad, "tensor", 1)
+    g_core = swap(output_grad, "tensor", 0)
     g_both = swap(g_far, "tensor", 0)
 
     rows_wide, rows_low = ((rows, width), WIDE), ((rows, width), LOW)
     parts_outs = [rows_wide, rows_wide, rows_low, rows_low]
-    attn, totals, keep_near, keep_far, away_near, away_far = call(
+    head_parts = [((local, rows), LOW)] * 4
+    attn, totals, a0, b1, b2, b3 = call(
         attend_kernel,
-        [((local, length), LOW), ((heads, 1, length), WIDE)] + parts_outs,
-        mixed_near, mixed_far, seg_row, seg_col, proj_weight,
+        [((local, length), LOW), ((heads, 1, length), WIDE)] + head_parts,
+        mixed_near, mixed_far, seg_row, seg_col,
         scratch=[((heads, length, HD), LOW), ((local, length), LOW)],
         flops=16 * heads * length * length * HD,
     )
-    from_chip, from_core = reduce_parts(keep_far, away_far, away_near)
+    a1 = exchange(b1, "tensor", 1)
+    a2 = exchange(b2, "tensor", 2)
+    a3 = exchange(b3, "tensor", 3)
     mid, n0 = call(
         middle_kernel, [rows_wide, rows_low],
-        block_input, keep_near, from_core, from_chip, gain_b,
+        block_input, a0, a1, a2, a3, w0, w1, w2, w3, gain_b,
     )
     n2 = swap(n0, "tensor", 1)
     n1 = swap(n0, "tensor", 0)
@@ -489,13 +504,19 @@
         flops=ff_flops,
     )
     from_chip, from_core = reduce_parts(keep_far, away_far, away_near)
-    grad_mid, m0 = call(
-        middle_back_kernel, [rows_wide, rows_low],
-        mid, output_grad, keep_near, from_core, from_chip, gain_b,
-    )
-    m2 = swap(m0, "tensor", 1)
-    m1 = swap(m0, "tensor", 0)
-    m3 = swap(m2, "tensor", 0)
+    grad_mid, m0, h0, e1, e2, e3 = call(
+        middle_back_kernel, [rows_wide, rows_low] + head_parts,
+        mid, output_grad, keep_near, from_core, from_chip, gain_b, w0, w1, w2, w3,
+    )
+    h1 = exchange(e1, "tensor", 1)
+    h2 = exchange(e2, "tensor", 2)
+    h3 = exchange(e3, "tensor", 3)
+    head_wide, head_low = ((local, width), WIDE), ((local, width), LOW)
+    proj_keep, proj_far, proj_away_near, proj_away_far = call(
+        proj_grad_kernel, [head_wide, head_wide, head_low, head_low],
+        a0, a1, a2, a3, m0, flops=2 * length * width * local,
+    )
+    proj_chip, proj_core = reduce_parts(proj_far, proj_away_far, proj_away_near)
 
     order = list(bits_of("dp"))
     turned_order = order[1:] + order[:1]
@@ -506,7 +527,7 @@
         functools.partial(wide_grad_kernel, bits=firsts),
         [(pieces, WIDE), (pieces, LOW), (pieces, WIDE), (pieces, LOW)],
         own, dgate_near, dup_near, act_near, dgate_far, dup_far, act_far,
-        n0, output_grad, n1, g_core, n2, g_far, n3, g_both, streamed=True, limit=56,
+        n0, output_grad, n1, g_core, n2, g_far, n3, g_both, streamed=True, limit=52,
         scratch=[((blocks, width // blocks, units), WIDE)],
         scalars=1, flops=2 * length * width * units * 3,
     )
@@ -530,7 +551,7 @@
     grad_mixed, keep_near, keep_far, away_near, away_far, gain_part_one = call(
         attend_back_kernel,
         [((3 * local, length), LOW)] + parts_outs + [gain_row],
-        mixed_near, mixed_far, attn, totals, m0, m1, m2, m3, proj_weight, seg_row, seg_col,
+        mixed_near, mixed_far, attn, totals, h0, h1, h2, h3, seg_row, seg_col,
         cosine, sine, turned, rows_near, rows_far,
         scratch=[((length, HD), LOW), ((length, HD), LOW), ((local, length), LOW),
                  ((HD, length), WIDE), ((HD, length), WIDE)],
@@ -541,7 +562,7 @@
     kept_a, away_a, kept_b, away_b = call(
         functools.partial(qkv_grad_kernel, bits=firsts),
         [(pieces, WIDE), (pieces, LOW), (pieces, WIDE), (pieces, LOW)],
-        own, normed_near, normed_far, grad_mixed, m0, m1, m2, m3, attn,
+        own, normed_near, normed_far, grad_mixed, proj_keep, proj_core, proj_chip,
         scalars=1, flops=2 * length * width * local * 4,
         scratch=[((blocks, width // blocks, 2 * local), WIDE)],
     )

time: 176 us -> 180 us (1.023)
  waiting for transfers between devices: 71.5 us -> 73.4 us
  starting transfers between devices: 39.5 us -> 41.4 us
    ppermute x41 -> x47, starting transfers between devices: 39.5 us -> 41.4 us  [exchange(): return lax.ppermute(values_in, axis, [(i, i ^ mask) for i in range(size)])]
    ppermute x41 -> x47, waiting for transfers between devices: 71.5 us -> 73.4 us  [exchange(): return lax.ppermute(values_in, axis, [(i, i ^ mask) for i in range(size)])]
    pallas_call x15 -> x16, Pallas kernels: 48.1 us -> 47.5 us  [call(): pl.pallas_call(kernel, out_shape=shapes, in_specs=spaces, out_specs=[pl.B...]
    unnamed x75 -> x93, local copies, waits for them, and re-layouts: 11 us -> 11.2 us
  transfers between devices with their start and end apart: 41 -> 47, of which waited for: 15 -> 24; matrix products, arithmetic and copies ran while one was open for 3% -> 3% of each run, Pallas kernels for 14% -> 20%
where the time goes in v1:
time: 180 us; the launch traced here: 179 us
  waiting for transfers between devices  73.4 us (41%)
  Pallas kernels  47.5 us (26%)
  starting transfers between devices  41.4 us (23%)
  local copies, waits for them, and re-layouts  13.4 us (7%)
  other arithmetic  2.2 us (1%)
    ppermute x47, waiting for transfers between devices, exchange(): return lax.ppermute(values_in, axis, [(i, i ^ mask) for i in range(size)])  73.4 us
    pallas_call x16, Pallas kernels, call(): pl.pallas_call(kernel, out_shape=shapes, in_specs=spaces, out_specs=[pl.B...  47.5 us
    ppermute x47, starting transfers between devices, exchange(): return lax.ppermute(values_in, axis, [(i, i ^ mask) for i in range(size)])  41.4 us
    unnamed x93, local copies, waits for them, and re-layouts  11.2 us
  transfers between devices with their start and end apart: 47, of which 24 were waited for; matrix products, arithmetic and copies ran while one was open for 3% of the time, Pallas kernels for 20%

profile of v1, /device:TPU:0, one launch (start us, length us, event | category | flops | bytes accessed | tf_op | source)
XLA Modules:
  0.0 179.2 jit_solution(11911009795210186418)
XLA Ops:
  0.6 3.0 %collective-permute-start.1 = (bf16[256,768]{1,0:T(8,128)(2,1)}, bf16[256,768]{1,0:T(8,128)(2,1)S(1)}, u32[]{:S(2)}, u32[]{:S(2)}) collective-permute-start(bf16[256,768]{1,0:T(8,128)(2,1)} %x_ref.3), channel_id=1, source_target_pairs={{0,2},{1,3},{2,0},{3,1},{4,6},{5,7},{6,4},{7,5},{8,10},{9,11},{10,... | collective-permute-start | bytes 1179656 | tf_op jit(solution)/shard_map/ppermute | solution.py:29
  3.7 9.3 %collective-permute-done.1.near_ref = bf16[256,768]{1,0:T(8,128)(2,1)S(1)} collective-permute-done((bf16[256,768]{1,0:T(8,128)(2,1)}, bf16[256,768]{1,0:T(8,128)(2,1)S(1)}, u32[]{:S(2)}, u32[]{:S(2)}) %collective-permute-start.1) | collective-permute-done | bytes 393248 | tf_op jit(solution)/shard_map/ppermute | solution.py:29
  17.5 5.1 %collective-permute-done.7.w2 = bf16[192,768]{1,0:T(8,128)(2,1)S(1)} collective-permute-done((bf16[192,768]{1,0:T(8,128)(2,1)}, bf16[192,768]{1,0:T(8,128)(2,1)S(1)}, u32[]{:S(2)}, u32[]{:S(2)}) %collective-permute-start.7) | collective-permute-done | bytes 294944 | tf_op jit(solution)/shard_map/ppermute | solution.py:29
  30.6 8.5 %shard_map.156 = (bf16[192,1024]{1,0:T(8,128)(2,1)S(1)}, f32[3,1,1024]{2,1,0:T(1,128)S(1)}, bf16[192,256]{1,0:T(8,128)(2,1)S(1)}, bf16[192,256]{1,0:T(8,128)(2,1...) custom-call(bf16[576,512]{1,0:T(8,128)(2,1)S(1)} %get-tuple-element.71.near_ref, ...), custom_call_target="tpu_custom_call" | custom-call | flops 3221225472 | bytes 1708032 | tf_op jit(solution)/shard_map/pallas_call | solution.py:68
  45.3 2.1 %collective-permute-done.5.a3 = bf16[192,256]{1,0:T(8,128)(2,1)S(1)} collective-permute-done((bf16[192,256]{1,0:T(8,128)(2,1)S(1)}, bf16[192,256]{1,0:T(8,128)(2,1)S(1)}, u32[]{:S(2)}, u32[]{:S(2)}) %collective-permute-start.5) | collective-permute-done | bytes 98336 | tf_op jit(solution)/shard_map/ppermute | solution.py:29
  51.0 4.8 %collective-permute-done.13.grad_near_ref.refs_11_ = bf16[256,768]{1,0:T(8,128)(2,1)} collective-permute-done((bf16[256,768]{1,0:T(8,128)(2,1)S(1)}, bf16[256,768]{1,0:T(8,128)(2,1)}, u32[]{:S(2)}, u32[]{:S(2)}) %collective-permute-start.13) | collective-permute-done | bytes 393248 | tf_op jit(solution)/shard_map/ppermute | solution.py:29
  55.9 8.3 %collective-permute-done.11.near_ref.refs_10_ = bf16[256,768]{1,0:T(8,128)(2,1)} collective-permute-done((bf16[256,768]{1,0:T(8,128)(2,1)}, bf16[256,768]{1,0:T(8,128)(2,1)}, u32[]{:S(2)}, u32[]{:S(2)}) %collective-permute-start.11) | collective-permute-done | bytes 393248 | tf_op jit(solution)/shard_map/ppermute | solution.py:29
  65.6 4.0 %shard_map.158 = (bf16[512,288]{1,0:T(8,128)(2,1)S(1)}, bf16[512,288]{1,0:T(8,128)(2,1)S(1)}, bf16[512,288]{1,0:T(8,128)(2,1)S(1)}, f32[256,768]{1,0:T(8,128)S(1...) custom-call(bf16[256,768]{1,0:T(8,128)(2,1)} %get-tuple-element.80.near_ref.refs_6_, ...), custom_call_target="tpu_custom_call" | custom-call | flops 1358954496 | bytes 2899968 | tf_op jit(solution)/shard_map/pallas_call | solution.py:68
  69.6 3.9 %shard_map.159 = (bf16[512,288]{1,0:T(8,128)(2,1)S(1)}, bf16[512,288]{1,0:T(8,128)(2,1)S(1)}, bf16[512,288]{1,0:T(8,128)(2,1)S(1)}, f32[256,768]{1,0:T(8,128)S(1...) custom-call(bf16[256,768]{1,0:T(8,128)(2,1)} %collective-permute-done.11.near_ref.refs_10_, ...), custom_call_target="tpu_custom_call" | custom-call | flops 1358954496 | bytes 2899968 | tf_op jit(solution)/shard_map/pallas_call | solution.py:68
  75.9 7.2 %shard_map.167 = (f32[4,48,864]{2,1,0:T(8,128)}, bf16[4,48,864]{2,1,0:T(8,128)(2,1)S(1)}, f32[4,48,864]{2,1,0:T(8,128)}, bf16[4,48,864]{2,1,0:T(8,128)(2,1)S(1)}) custom-call(s32[1]{0:T(128)} %bitcast.10.own_ref, bf16[512,288]{1,0:T(8,128)(2,1)S(1)} %get-tuple-element.118.refs_0_, bf16[512,288]{1,0:T(8,128)(2,1)S(1)} %get-tuple-element.119.refs_1_, ...), custom_call_target="tpu_custom_call" | custom-call | flops 1358954496 | bytes 4915204 | tf_op jit(solution)/shard_map/pallas_call | solution.py:68
  88.1 5.6 %collective-permute-done.39 = bf16[4,48,864]{2,1,0:T(8,128)(2,1)S(1)} collective-permute-done((bf16[4,48,864]{2,1,0:T(8,128)(2,1)S(1)}, bf16[4,48,864]{2,1,0:T(8,128)(2,1)S(1)}, u32[]{:S(2)}, u32[]{:S(2)}) %collective-permute-start.39) | collective-permute-done | bytes 331808 | tf_op jit(solution)/shard_map/ppermute | solution.py:29
  95.6 2.6 %collective-permute-start.40 = (bf16[2,48,864]{2,1,0:T(8,128)(2,1)S(1)}, bf16[2,48,864]{2,1,0:T(8,128)(2,1)S(1)}, u32[]{:S(2)}, u32[]{:S(2)}) collective-permute-start(bf16[2,48,864]{2,1,0:T(8,128)(2,1)S(1)} %slice.122), channel_id=1, source_target_pairs={{0,16},{4,20},{8,24},{12,28},{16,0},{20,4},{24,8},{28,12},{1,17},{... | collective-permute-start | bytes 497672 | tf_op jit(solution)/shard_map/ppermute | solution.py:29
  100.6 5.3 %collective-permute-done.40 = bf16[2,48,864]{2,1,0:T(8,128)(2,1)S(1)} collective-permute-done((bf16[2,48,864]{2,1,0:T(8,128)(2,1)S(1)}, bf16[2,48,864]{2,1,0:T(8,128)(2,1)S(1)}, u32[]{:S(2)}, u32[]{:S(2)}) %collective-permute-start.40) | collective-permute-done | bytes 165920 | tf_op jit(solution)/shard_map/ppermute | solution.py:29
  107.5 3.4 %collective-permute-done.20.chip_ref = bf16[256,768]{1,0:T(8,128)(2,1)S(1)} collective-permute-done((bf16[256,768]{1,0:T(8,128)(2,1)S(1)}, bf16[256,768]{1,0:T(8,128)(2,1)S(1)}, u32[]{:S(2)}, u32[]{:S(2)}) %collective-permute-start.20) | collective-permute-done | bytes 393248 | tf_op jit(solution)/shard_map/ppermute | solution.py:29
  115.7 5.3 %collective-permute-done.22.g2 = bf16[192,256]{1,0:T(8,128)(2,1)S(1)} collective-permute-done((bf16[192,256]{1,0:T(8,128)(2,1)S(1)}, bf16[192,256]{1,0:T(8,128)(2,1)S(1)}, u32[]{:S(2)}, u32[]{:S(2)}) %collective-permute-start.22) | collective-permute-done | bytes 98336 | tf_op jit(solution)/shard_map/ppermute | solution.py:29
  121.2 12.0 %shard_map.162 = (bf16[576,1024]{1,0:T(8,128)(2,1)S(1)}, f32[256,768]{1,0:T(8,128)S(1)}, f32[256,768]{1,0:T(8,128)S(1)}, bf16[256,768]{1,0:T(8,128)(2,1)S(1)}, b...) custom-call(bf16[576,512]{1,0:T(8,128)(2,1)S(1)} %copy-done.34, bf16[576,512]{1,0:T(8,128)(2,1)S(1)} %copy-done.36, ...), custom_call_target="tpu_custom_call" | custom-call | flops 8053063680 | bytes 5226496 | tf_op jit(solution)/shard_map/pallas_call | solution.py:68
  136.5 2.1 %collective-permute-done.43 = f32[2,768]{1,0:T(2,128)S(1)} collective-permute-done((f32[2,768]{1,0:T(2,128)S(1)}, f32[2,768]{1,0:T(2,128)S(1)}, u32[]{:S(2)}, u32[]{:S(2)}) %collective-permute-start.43) | collective-permute-done | bytes 6176 | tf_op jit(solution)/shard_map/ppermute | solution.py:29
  140.7 1.9 %collective-permute-done.44 = f32[2,768]{1,0:T(2,128)S(1)} collective-permute-done((f32[2,768]{1,0:T(2,128)S(1)}, f32[2,768]{1,0:T(2,128)S(1)}, u32[]{:S(2)}, u32[]{:S(2)}) %collective-permute-start.44) | collective-permute-done | bytes 6176 | tf_op jit(solution)/shard_map/ppermute | solution.py:29
  148.6 1.9 %collective-permute-start.46 = (f32[2,768]{1,0:T(2,128)S(1)}, f32[2,768]{1,0:T(2,128)S(1)}, u32[]{:S(2)}, u32[]{:S(2)}) collective-permute-start(f32[2,768]{1,0:T(2,128)S(1)} %add.82), channel_id=1, source_target_pairs={{0,16},{4,20},{8,24},{12,28},{16,0},{20,4},{24,8},{28,12},{1,17},{... | collective-permute-start | bytes 18440 | tf_op jit(solution)/shard_map/ppermute | solution.py:29
  157.9 3.6 %collective-permute-done.33 = bf16[4,96,384]{2,1,0:T(8,128)(2,1)S(1)} collective-permute-done((bf16[4,96,384]{2,1,0:T(8,128)(2,1)S(1)}, bf16[4,96,384]{2,1,0:T(8,128)(2,1)S(1)}, u32[]{:S(2)}, u32[]{:S(2)}) %collective-permute-start.33) | collective-permute-done | bytes 294944 | tf_op jit(solution)/shard_map/ppermute | solution.py:29
  162.7 2.2 %collective-permute-done.30 = bf16[4,96,384]{2,1,0:T(8,128)(2,1)S(1)} collective-permute-done((bf16[4,96,384]{2,1,0:T(8,128)(2,1)S(1)}, bf16[4,96,384]{2,1,0:T(8,128)(2,1)S(1)}, u32[]{:S(2)}, u32[]{:S(2)}) %collective-permute-start.30) | collective-permute-done | bytes 294944 | tf_op jit(solution)/shard_map/ppermute | solution.py:29
  165.5 2.2 %collective-permute-done.26.chip_ref = bf16[256,768]{1,0:T(8,128)(2,1)S(1)} collective-permute-done((bf16[256,768]{1,0:T(8,128)(2,1)S(1)}, bf16[256,768]{1,0:T(8,128)(2,1)S(1)}, u32[]{:S(2)}, u32[]{:S(2)}) %collective-permute-start.26) | collective-permute-done | bytes 393248 | tf_op jit(solution)/shard_map/ppermute | solution.py:29
  172.9 2.1 %collective-permute-done.35.came_b = bf16[96,384]{1,0:T(8,128)(2,1)S(1)} collective-permute-done((bf16[96,384]{1,0:T(8,128)(2,1)S(1)}, bf16[96,384]{1,0:T(8,128)(2,1)S(1)}, u32[]{:S(2)}, u32[]{:S(2)}) %collective-permute-start.35) | collective-permute-done | bytes 73760 | tf_op jit(solution)/shard_map/ppermute | solution.py:29
  175.0 3.3 %collective-permute-done.32.came_a = bf16[96,384]{1,0:T(8,128)(2,1)S(1)} collective-permute-done((bf16[96,384]{1,0:T(8,128)(2,1)S(1)}, bf16[96,384]{1,0:T(8,128)(2,1)S(1)}, u32[]{:S(2)}, u32[]{:S(2)}) %collective-permute-start.32) | collective-permute-done | bytes 73760 | tf_op jit(solution)/shard_map/ppermute | solution.py:29
  (215 shorter events, 68.0 us)
Async XLA Ops:
  0.6 12.4 %collective-permute-start.1 = (bf16[256,768]{1,0:T(8,128)(2,1)}, bf16[256,768]{1,0:T(8,128)(2,1)S(1)}, u32[]{:S(2)}, u32[]{:S(2)}) collective-permute-start(bf16[256,768]{1,0:T(8,128)(2,1)} %x_ref.3), channel_id=1, source_target_pairs={{0,2},{1,3},{2,0},{3,1},{4,6},{5,7},{6,4},{7,5},{8,10},{9,11},{10,... | collective-permute-start | bytes 1179656 | tf_op jit(solution)/shard_map/ppermute | solution.py:29
  3.7 19.0 %collective-permute-start = (bf16[256,768]{1,0:T(8,128)(2,1)}, bf16[256,768]{1,0:T(8,128)(2,1)S(1)}, u32[]{:S(2)}, u32[]{:S(2)}) collective-permute-start(bf16[256,768]{1,0:T(8,128)(2,1)} %x_ref.3), channel_id=1, source_target_pairs={{0,1},{1,0},{2,3},{3,2},{4,5},{5,4},{6,7},{7,6},{8,9},{9,8},{10,11... | collective-permute-start | bytes 1179656 | tf_op jit(solution)/shard_map/ppermute | solution.py:29
  13.0 14.7 %collective-permute-start.2 = (bf16[256,768]{1,0:T(8,128)(2,1)S(1)}, bf16[256,768]{1,0:T(8,128)(2,1)S(1)}, u32[]{:S(2)}, u32[]{:S(2)}) collective-permute-start(bf16[256,768]{1,0:T(8,128)(2,1)S(1)} %collective-permute-done.1.near_ref), channel_id=1, source_target_pairs={{0,1},{1,0},{2,3},{3,2},{4,5},{5,4},{6,7},{7,6},{8,9},{9,8},{10,11... | collective-permute-start | bytes 1179656 | tf_op jit(solution)/shard_map/ppermute | solution.py:29
  13.0 9.6 %collective-permute-start.7 = (bf16[192,768]{1,0:T(8,128)(2,1)}, bf16[192,768]{1,0:T(8,128)(2,1)S(1)}, u32[]{:S(2)}, u32[]{:S(2)}) collective-permute-start(bf16[192,768]{1,0:T(8,128)(2,1)} %w0.3), channel_id=1, source_target_pairs={{0,2},{1,3},{2,0},{3,1},{4,6},{5,7},{6,4},{7,5},{8,10},{9,11},{10,... | collective-permute-start | bytes 884744 | tf_op jit(solution)/shard_map/ppermute | solution.py:29
  14.7 27.4 %collective-permute-start.6 = (bf16[192,768]{1,0:T(8,128)(2,1)}, bf16[192,768]{1,0:T(8,128)(2,1)S(1)}, u32[]{:S(2)}, u32[]{:S(2)}) collective-permute-start(bf16[192,768]{1,0:T(8,128)(2,1)} %w0.3), channel_id=1, source_target_pairs={{0,1},{1,0},{2,3},{3,2},{4,5},{5,4},{6,7},{7,6},{8,9},{9,8},{10,11... | collective-permute-start | bytes 884744 | tf_op jit(solution)/shard_map/ppermute | solution.py:29
  22.6 20.9 %collective-permute-start.8 = (bf16[192,768]{1,0:T(8,128)(2,1)S(1)}, bf16[192,768]{1,0:T(8,128)(2,1)S(1)}, u32[]{:S(2)}, u32[]{:S(2)}) collective-permute-start(bf16[192,768]{1,0:T(8,128)(2,1)S(1)} %collective-permute-done.7.w2), channel_id=1, source_target_pairs={{0,1},{1,0},{2,3},{3,2},{4,5},{5,4},{6,7},{7,6},{8,9},{9,8},{10,11... | collective-permute-start | bytes 884744 | tf_op jit(solution)/shard_map/ppermute | solution.py:29
  42.1 13.7 %collective-permute-start.13 = (bf16[256,768]{1,0:T(8,128)(2,1)S(1)}, bf16[256,768]{1,0:T(8,128)(2,1)}, u32[]{:S(2)}, u32[]{:S(2)}) collective-permute-start(bf16[256,768]{1,0:T(8,128)(2,1)S(1)} %copy-done.4), channel_id=1, source_target_pairs={{0,2},{1,3},{2,0},{3,1},{4,6},{5,7},{6,4},{7,5},{8,10},{9,11},{10,... | collective-permute-start | bytes 1179656 | tf_op jit(solution)/shard_map/ppermute | solution.py:29
  49.0 15.1 %collective-permute-start.11 = (bf16[256,768]{1,0:T(8,128)(2,1)}, bf16[256,768]{1,0:T(8,128)(2,1)}, u32[]{:S(2)}, u32[]{:S(2)}) collective-permute-start(bf16[256,768]{1,0:T(8,128)(2,1)} %get-tuple-element.80.near_ref.refs_6_), channel_id=1, source_target_pairs={{0,2},{1,3},{2,0},{3,1},{4,6},{5,7},{6,4},{7,5},{8,10},{9,11},{10,... | collective-permute-start | bytes 1179656 | tf_op jit(solution)/shard_map/ppermute | solution.py:29
  49.5 16.1 %collective-permute-start.10 = (bf16[256,768]{1,0:T(8,128)(2,1)S(1)}, bf16[256,768]{1,0:T(8,128)(2,1)}, u32[]{:S(2)}, u32[]{:S(2)}) collective-permute-start(bf16[256,768]{1,0:T(8,128)(2,1)S(1)} %copy-done.4), channel_id=1, source_target_pairs={{0,1},{1,0},{2,3},{3,2},{4,5},{5,4},{6,7},{7,6},{8,9},{9,8},{10,11... | collective-permute-start | bytes 1179656 | tf_op jit(solution)/shard_map/ppermute | solution.py:29
  51.0 14.6 %collective-permute-start.9 = (bf16[256,768]{1,0:T(8,128)(2,1)}, bf16[256,768]{1,0:T(8,128)(2,1)}, u32[]{:S(2)}, u32[]{:S(2)}) collective-permute-start(bf16[256,768]{1,0:T(8,128)(2,1)} %get-tuple-element.80.near_ref.refs_6_), channel_id=1, source_target_pairs={{0,1},{1,0},{2,3},{3,2},{4,5},{5,4},{6,7},{7,6},{8,9},{9,8},{10,11... | collective-permute-start | bytes 1179656 | tf_op jit(solution)/shard_map/ppermute | solution.py:29
  55.8 13.8 %collective-permute-start.14 = (bf16[256,768]{1,0:T(8,128)(2,1)}, bf16[256,768]{1,0:T(8,128)(2,1)}, u32[]{:S(2)}, u32[]{:S(2)}) collective-permute-start(bf16[256,768]{1,0:T(8,128)(2,1)} %collective-permute-done.13.grad_near_ref.refs_11_), channel_id=1, source_target_pairs={{0,1},{1,0},{2,3},{3,2},{4,5},{5,4},{6,7},{7,6},{8,9},{9,8},{10,11... | collective-permute-start | bytes 1179656 | tf_op jit(solution)/shard_map/ppermute | solution.py:29
  83.1 10.5 %collective-permute-start.39 = (bf16[4,48,864]{2,1,0:T(8,128)(2,1)S(1)}, bf16[4,48,864]{2,1,0:T(8,128)(2,1)S(1)}, u32[]{:S(2)}, u32[]{:S(2)}) collective-permute-start(bf16[4,48,864]{2,1,0:T(8,128)(2,1)S(1)} %get-tuple-element.125), channel_id=1, source_target_pairs={{0,8},{4,12},{8,0},{12,4},{16,24},{20,28},{24,16},{28,20},{1,9},{5... | collective-permute-start | bytes 995336 | tf_op jit(solution)/shard_map/ppermute | solution.py:29
  84.9 22.6 %collective-permute-start.18 = (bf16[256,768]{1,0:T(8,128)(2,1)S(1)}, bf16[256,768]{1,0:T(8,128)(2,1)S(1)}, u32[]{:S(2)}, u32[]{:S(2)}) collective-permute-start(bf16[256,768]{1,0:T(8,128)(2,1)S(1)} %get-tuple-element.88), channel_id=1, source_target_pairs={{0,1},{1,0},{2,3},{3,2},{4,5},{5,4},{6,7},{7,6},{8,9},{9,8},{10,11... | collective-permute-start | bytes 1179656 | tf_op jit(solution)/shard_map/ppermute | solution.py:29
  85.1 13.2 %collective-permute-start.19 = (bf16[256,768]{1,0:T(8,128)(2,1)S(1)}, bf16[256,768]{1,0:T(8,128)(2,1)S(1)}, u32[]{:S(2)}, u32[]{:S(2)}) collective-permute-start(bf16[256,768]{1,0:T(8,128)(2,1)S(1)} %get-tuple-element.90), channel_id=1, source_target_pairs={{0,1},{1,0},{2,3},{3,2},{4,5},{5,4},{6,7},{7,6},{8,9},{9,8},{10,11... | collective-permute-start | bytes 1179656 | tf_op jit(solution)/shard_map/ppermute | solution.py:29
  85.4 10.2 %collective-permute-start.36 = (bf16[4,48,864]{2,1,0:T(8,128)(2,1)S(1)}, bf16[4,48,864]{2,1,0:T(8,128)(2,1)S(1)}, u32[]{:S(2)}, u32[]{:S(2)}) collective-permute-start(bf16[4,48,864]{2,1,0:T(8,128)(2,1)S(1)} %get-tuple-element.123), channel_id=1, source_target_pairs={{0,4},{4,0},{8,12},{12,8},{16,20},{20,16},{24,28},{28,24},{1,5},{5... | collective-permute-start | bytes 995336 | tf_op jit(solution)/shard_map/ppermute | solution.py:29
  88.0 10.9 %collective-permute-start.16 = (bf16[256,768]{1,0:T(8,128)(2,1)S(1)}, bf16[256,768]{1,0:T(8,128)(2,1)S(1)}, u32[]{:S(2)}, u32[]{:S(2)}) collective-permute-start(bf16[256,768]{1,0:T(8,128)(2,1)S(1)} %get-tuple-element.86), channel_id=1, source_target_pairs={{0,1},{1,0},{2,3},{3,2},{4,5},{5,4},{6,7},{7,6},{8,9},{9,8},{10,11... | collective-permute-start | bytes 1179656 | tf_op jit(solution)/shard_map/ppermute | solution.py:29
  93.6 60.3 %collective-permute-start.15 = (bf16[256,768]{1,0:T(8,128)(2,1)S(1)}, bf16[256,768]{1,0:T(8,128)(2,1)S(1)}, u32[]{:S(2)}, u32[]{:S(2)}) collective-permute-start(bf16[256,768]{1,0:T(8,128)(2,1)S(1)} %get-tuple-element.84), channel_id=1, source_target_pairs={{0,1},{1,0},{2,3},{3,2},{4,5},{5,4},{6,7},{7,6},{8,9},{9,8},{10,11... | collective-permute-start | bytes 1179656 | tf_op jit(solution)/shard_map/ppermute | solution.py:29
  95.6 10.3 %collective-permute-start.40 = (bf16[2,48,864]{2,1,0:T(8,128)(2,1)S(1)}, bf16[2,48,864]{2,1,0:T(8,128)(2,1)S(1)}, u32[]{:S(2)}, u32[]{:S(2)}) collective-permute-start(bf16[2,48,864]{2,1,0:T(8,128)(2,1)S(1)} %slice.122), channel_id=1, source_target_pairs={{0,16},{4,20},{8,24},{12,28},{16,0},{20,4},{24,8},{28,12},{1,17},{... | collective-permute-start | bytes 497672 | tf_op jit(solution)/shard_map/ppermute | solution.py:29
  98.9 12.1 %collective-permute-start.20 = (bf16[256,768]{1,0:T(8,128)(2,1)S(1)}, bf16[256,768]{1,0:T(8,128)(2,1)S(1)}, u32[]{:S(2)}, u32[]{:S(2)}) collective-permute-start(bf16[256,768]{1,0:T(8,128)(2,1)S(1)} %add_convert_fusion.1), channel_id=1, source_target_pairs={{0,2},{1,3},{2,0},{3,1},{4,6},{5,7},{6,4},{7,5},{8,10},{9,11},{10,... | collective-permute-start | bytes 1179656 | tf_op jit(solution)/shard_map/ppermute | solution.py:29
  105.9 48.0 %collective-permute-start.17 = (bf16[256,768]{1,0:T(8,128)(2,1)S(1)}, bf16[256,768]{1,0:T(8,128)(2,1)S(1)}, u32[]{:S(2)}, u32[]{:S(2)}) collective-permute-start(bf16[256,768]{1,0:T(8,128)(2,1)S(1)} %add_convert_fusion.3), channel_id=1, source_target_pairs={{0,2},{1,3},{2,0},{3,1},{4,6},{5,7},{6,4},{7,5},{8,10},{9,11},{10,... | collective-permute-start | bytes 1179656 | tf_op jit(solution)/shard_map/ppermute | solution.py:29
  114.1 26.5 %collective-permute-start.41 = (bf16[48,864]{1,0:T(8,128)(2,1)S(1)}, bf16[48,864]{1,0:T(8,128)(2,1)S(1)}, u32[]{:S(2)}, u32[]{:S(2)}) collective-permute-start(bf16[48,864]{1,0:T(8,128)(2,1)S(1)} %fusion.5), channel_id=1, source_target_pairs={{0,4},{4,0},{8,12},{12,8},{16,20},{20,16},{24,28},{28,24},{1,5},{5... | collective-permute-start | bytes 248840 | tf_op jit(solution)/shard_map/ppermute | solution.py:29
  154.8 10.6 %collective-permute-start.24 = (bf16[256,768]{1,0:T(8,128)(2,1)S(1)}, bf16[256,768]{1,0:T(8,128)(2,1)S(1)}, u32[]{:S(2)}, u32[]{:S(2)}) collective-permute-start(bf16[256,768]{1,0:T(8,128)(2,1)S(1)} %get-tuple-element.101), channel_id=1, source_target_pairs={{0,1},{1,0},{2,3},{3,2},{4,5},{5,4},{6,7},{7,6},{8,9},{9,8},{10,11... | collective-permute-start | bytes 1179656 | tf_op jit(solution)/shard_map/ppermute | solution.py:29
  155.4 9.4 %collective-permute-start.30 = (bf16[4,96,384]{2,1,0:T(8,128)(2,1)S(1)}, bf16[4,96,384]{2,1,0:T(8,128)(2,1)S(1)}, u32[]{:S(2)}, u32[]{:S(2)}) collective-permute-start(bf16[4,96,384]{2,1,0:T(8,128)(2,1)S(1)} %get-tuple-element.113), channel_id=1, source_target_pairs={{0,4},{4,0},{8,12},{12,8},{16,20},{20,16},{24,28},{28,24},{1,5},{5... | collective-permute-start | bytes 884744 | tf_op jit(solution)/shard_map/ppermute | solution.py:29
  156.4 11.3 %collective-permute-start.26 = (bf16[256,768]{1,0:T(8,128)(2,1)S(1)}, bf16[256,768]{1,0:T(8,128)(2,1)S(1)}, u32[]{:S(2)}, u32[]{:S(2)}) collective-permute-start(bf16[256,768]{1,0:T(8,128)(2,1)S(1)} %add_convert_fusion), channel_id=1, source_target_pairs={{0,2},{1,3},{2,0},{3,1},{4,6},{5,7},{6,4},{7,5},{8,10},{9,11},{10,... | collective-permute-start | bytes 1179656 | tf_op jit(solution)/shard_map/ppermute | solution.py:29
  (69 other events, 542.6 us)

commit v2 on v1

--- a/solution.py
+++ b/solution.py
@@ -55,14 +55,10 @@
     return kept.reshape(kept.shape[-2:]), came.reshape(kept.shape[-2:])
 
 
-def call(kernel, outs, *operands, scalars=0, flops=0, scratch=(), limit=20, streamed=False):
+def call(kernel, outs, *operands, scalars=0, flops=0, scratch=(), limit=20):
     spaces = [pl.BlockSpec(memory_space=pltpu.SMEM)] * scalars
-    space = pltpu.HBM if streamed else pltpu.VMEM
-    spaces += [pl.BlockSpec(memory_space=space)] * (len(operands) - scalars)
+    spaces += [pl.BlockSpec(memory_space=pltpu.VMEM)] * (len(operands) - scalars)
     held = [pltpu.VMEM(shape, kind) for shape, kind in scratch]
-    if streamed:
-        held += [pltpu.VMEM(x.shape, x.dtype) for x in operands[scalars:]]
-        held += [pltpu.SemaphoreType.DMA((len(operands) - scalars,))]
     moved = sum(x.size * x.dtype.itemsize for x in operands)
     shapes = [jax.ShapeDtypeStruct(shape, kind) for shape, kind in outs]
     return pl.pallas_call(
@@ -250,38 +246,41 @@
         away_ref[index, :, columns] = away[top : top + rows].astype(LOW)
 
 
-def wide_grad_kernel(own_ref, *refs, bits):
-    count = 14
-    kept_a, away_a, kept_b, away_b = refs[count : count + 4]
-    total_ref = refs[count + 4]
-    held = refs[count + 5 : 2 * count + 5]
-    semaphores = refs[2 * count + 5]
-    copies = [
-        pltpu.make_async_copy(refs[index], held[index], semaphores.at[index])
-        for index in range(count)
-    ]
-    for copy in copies:
-        copy.start()
-    rows = held[6].shape[0]
-    units = held[0].shape[1]
+def wide_sums(n0, n1, g0, g1, dgate_ref, dup_ref, act_ref):
+    rows = n0.shape[0]
     sums = [None, None, None]
-    for place in range(4):
-        if place % 2 == 0:
-            for copy in copies[3 * (place // 2) : 3 * (place // 2) + 3]:
-                copy.wait()
-        for copy in copies[6 + 2 * place : 8 + 2 * place]:
-            copy.wait()
-        at = slice(place % 2 * rows, (place % 2 + 1) * rows)
-        turned = held[6 + 2 * place][...].T
-        turned_grad = held[7 + 2 * place][...].T
-        for index, left in enumerate((turned, turned, turned_grad)):
-            more = dot(left, held[3 * (place // 2) + index][at, :])
+    for place, (normed, grad) in enumerate(((n0, g0), (n1, g1))):
+        at = slice(place * rows, (place + 1) * rows)
+        turned, turned_grad = normed[...].T, grad[...].T
+        for index, (left, ref) in enumerate(
+            ((turned, dgate_ref), (turned, dup_ref), (turned_grad, act_ref))
+        ):
+            more = dot(left, ref[at, :])
             sums[index] = more if sums[index] is None else sums[index] + more
+    return sums
+
+
+def wide_near_kernel(n0, n1, g0, g1, dgate_ref, dup_ref, act_ref, out_ref):
+    for index, total in enumerate(wide_sums(n0, n1, g0, g1, dgate_ref, dup_ref, act_ref)):
+        out_ref[index] = total
+
+
+def wide_far_kernel(
+    own_ref, n0, n1, g0, g1, dgate_ref, dup_ref, act_ref, near_ref,
+    kept_a, away_a, kept_b, away_b, total_ref, *, bits,
+):
     half_rows = kept_a.shape[1]
-    for index in range(3):
-        hold_blocks(sums[index], total_ref)
+    units = act_ref.shape[1]
+    for index, total in enumerate(wide_sums(n0, n1, g0, g1, dgate_ref, dup_ref, act_ref)):
+        hold_blocks(total + near_ref[index], total_ref)
         store_blocks(own_ref, kept_a, away_a, total_ref, bits[0], 0, index * units)
         store_blocks(own_ref, kept_b, away_b, total_ref, bits[1], half_rows, index * units)
+
+
+def block_kernel(mid_ref, keep_ref, core_ref, chip_ref, out_ref):
+    total = mid_ref[...] + keep_ref[...]
+    total = total + core_ref[...].astype(WIDE) + chip_ref[...].astype(WIDE)
+    out_ref[...] = total.astype(LOW)
 
 
 def attend_back_kernel(
@@ -498,6 +497,11 @@
         forward_kernel, ff_outs, n0, n1, output_grad, g_core, gate_w, up_w, down_weight,
         flops=ff_flops,
     )
+    (wide_part,) = call(
+        wide_near_kernel, [((3, width, units), WIDE)],
+        n0, n1, output_grad, g_core, dgate_near, dup_near, act_near,
+        flops=length * width * units * 3,
+    )
     n3 = swap(n2, "tensor", 0)
     dgate_far, dup_far, act_far, keep_far, away_far, gain_far = call(
         forward_kernel, ff_outs, n2, n3, g_far, g_both, gate_w, up_w, down_weight,
@@ -524,12 +528,11 @@
     half_rows = width // blocks // 2
     pieces = (blocks // 2, half_rows, 3 * units)
     kept_a, away_a, kept_b, away_b = call(
-        functools.partial(wide_grad_kernel, bits=firsts),
+        functools.partial(wide_far_kernel, bits=firsts),
         [(pieces, WIDE), (pieces, LOW), (pieces, WIDE), (pieces, LOW)],
-        own, dgate_near, dup_near, act_near, dgate_far, dup_far, act_far,
-        n0, output_grad, n1, g_core, n2, g_far, n3, g_both, streamed=True, limit=52,
+        own, n2, n3, g_far, g_both, dgate_far, dup_far, act_far, wide_part,
         scratch=[((blocks, width // blocks, units), WIDE)],
-        scalars=1, flops=2 * length * width * units * 3,
+        scalars=1, flops=length * width * units * 3, limit=57,
     )
     first = scatter_rows(kept_a, away_a, order)
     second = scatter_rows(kept_b, away_b, turned_order)
@@ -544,9 +547,7 @@
         flops=2 * length * width * units,
     )
     out_chip, out_core = reduce_parts(out_far, out_away_far, out_away_near)
-    block_output = (
-        mid + out_near + out_core.astype(WIDE) + out_chip.astype(WIDE)
-    ).astype(LOW)
+    (block_output,) = call(block_kernel, [rows_low], mid, out_near, out_core, out_chip)
 
     grad_mixed, keep_near, keep_far, away_near, away_far, gain_part_one = call(
         attend_back_kernel,

time: 180 us -> 191 us (1.061)
  local copies, waits for them, and re-layouts: 13.4 us -> 18.4 us
  starting transfers between devices: 41.4 us -> 46.3 us
  Pallas kernels: 47.5 us -> 51.3 us
  waiting for transfers between devices: 73.4 us -> 70.4 us
    unnamed x93 -> x91, local copies, waits for them, and re-layouts: 11.2 us -> 16.4 us
    ppermute x47, starting transfers between devices: 41.4 us -> 46.3 us  [exchange(): return lax.ppermute(values_in, axis, [(i, i ^ mask) for i in range(size)])]
    pallas_call x16 -> x18, Pallas kernels: 47.5 us -> 51.3 us  [call(): pl.pallas_call(kernel, out_shape=shapes, in_specs=spaces, out_specs=[pl.B...]
    ppermute x47, waiting for transfers between devices: 73.4 us -> 70.4 us  [exchange(): return lax.ppermute(values_in, axis, [(i, i ^ mask) for i in range(size)])]
  transfers between devices with their start and end apart: 47 -> 47, of which waited for: 24 -> 19; matrix products, arithmetic and copies ran while one was open for 3% -> 3% of each run, Pallas kernels for 20% -> 21%
where the time goes in v2:
time: 191 us; the launch traced here: 190 us
  waiting for transfers between devices  70.4 us (37%)
  Pallas kernels  51.3 us (27%)
  starting transfers between devices  46.3 us (24%)
  local copies, waits for them, and re-layouts  18.4 us (10%)
  other arithmetic  2.41 us (1%)
    ppermute x47, waiting for transfers between devices, exchange(): return lax.ppermute(values_in, axis, [(i, i ^ mask) for i in range(size)])  70.4 us
    pallas_call x18, Pallas kernels, call(): pl.pallas_call(kernel, out_shape=shapes, in_specs=spaces, out_specs=[pl.B...  51.3 us
    ppermute x47, starting transfers between devices, exchange(): return lax.ppermute(values_in, axis, [(i, i ^ mask) for i in range(size)])  46.3 us
    unnamed x91, local copies, waits for them, and re-layouts  16.4 us
  transfers between devices with their start and end apart: 47, of which 19 were waited for; matrix products, arithmetic and copies ran while one was open for 3% of the time, Pallas kernels for 21%

profile of v2, /device:TPU:0, one launch (start us, length us, event | category | flops | bytes accessed | tf_op | source)
XLA Modules:
  0.0 190.1 jit_solution(6403094500162084353)
XLA Ops:
  0.6 3.0 %collective-permute-start.1 = (bf16[256,768]{1,0:T(8,128)(2,1)}, bf16[256,768]{1,0:T(8,128)(2,1)S(1)}, u32[]{:S(2)}, u32[]{:S(2)}) collective-permute-start(bf16[256,768]{1,0:T(8,128)(2,1)} %x_ref.3), channel_id=1, source_target_pairs={{0,2},{1,3},{2,0},{3,1},{4,6},{5,7},{6,4},{7,5},{8,10},{9,11},{10,... | collective-permute-start | bytes 1179656 | tf_op jit(solution)/shard_map/ppermute | solution.py:29
  3.7 9.3 %collective-permute-done.1.near_ref = bf16[256,768]{1,0:T(8,128)(2,1)S(1)} collective-permute-done((bf16[256,768]{1,0:T(8,128)(2,1)}, bf16[256,768]{1,0:T(8,128)(2,1)S(1)}, u32[]{:S(2)}, u32[]{:S(2)}) %collective-permute-start.1) | collective-permute-done | bytes 393248 | tf_op jit(solution)/shard_map/ppermute | solution.py:29
  17.5 5.1 %collective-permute-done.7.w2 = bf16[192,768]{1,0:T(8,128)(2,1)S(1)} collective-permute-done((bf16[192,768]{1,0:T(8,128)(2,1)}, bf16[192,768]{1,0:T(8,128)(2,1)S(1)}, u32[]{:S(2)}, u32[]{:S(2)}) %collective-permute-start.7) | collective-permute-done | bytes 294944 | tf_op jit(solution)/shard_map/ppermute | solution.py:29
  32.0 8.5 %shard_map.156 = (bf16[192,1024]{1,0:T(8,128)(2,1)S(1)}, f32[3,1,1024]{2,1,0:T(1,128)S(1)}, bf16[192,256]{1,0:T(8,128)(2,1)S(1)}, bf16[192,256]{1,0:T(8,128)(2,1...) custom-call(bf16[576,512]{1,0:T(8,128)(2,1)S(1)} %get-tuple-element.71.near_ref, ...), custom_call_target="tpu_custom_call" | custom-call | flops 3221225472 | bytes 1708032 | tf_op jit(solution)/shard_map/pallas_call | solution.py:64
  46.7 2.1 %collective-permute-done.5.a3 = bf16[192,256]{1,0:T(8,128)(2,1)S(1)} collective-permute-done((bf16[192,256]{1,0:T(8,128)(2,1)S(1)}, bf16[192,256]{1,0:T(8,128)(2,1)S(1)}, u32[]{:S(2)}, u32[]{:S(2)}) %collective-permute-start.5) | collective-permute-done | bytes 98336 | tf_op jit(solution)/shard_map/ppermute | solution.py:29
  52.5 4.8 %collective-permute-done.13.grad_near_ref.g0 = bf16[256,768]{1,0:T(8,128)(2,1)S(1)} collective-permute-done((bf16[256,768]{1,0:T(8,128)(2,1)S(1)}, bf16[256,768]{1,0:T(8,128)(2,1)S(1)}, u32[]{:S(2)}, u32[]{:S(2)}) %collective-permute-start.13) | collective-permute-done | bytes 393248 | tf_op jit(solution)/shard_map/ppermute | solution.py:29
  57.3 8.3 %collective-permute-done.11.near_ref.n0 = bf16[256,768]{1,0:T(8,128)(2,1)} collective-permute-done((bf16[256,768]{1,0:T(8,128)(2,1)}, bf16[256,768]{1,0:T(8,128)(2,1)}, u32[]{:S(2)}, u32[]{:S(2)}) %collective-permute-start.11) | collective-permute-done | bytes 393248 | tf_op jit(solution)/shard_map/ppermute | solution.py:29
  67.9 4.7 %shard_map.158 = (bf16[512,288]{1,0:T(8,128)(2,1)S(1)}, bf16[512,288]{1,0:T(8,128)(2,1)S(1)}, bf16[512,288]{1,0:T(8,128)(2,1)S(1)}, f32[256,768]{1,0:T(8,128)S(1...) custom-call(bf16[256,768]{1,0:T(8,128)(2,1)} %get-tuple-element.80.near_ref.n0, ...), custom_call_target="tpu_custom_call" | custom-call | flops 1358954496 | bytes 2899968 | tf_op jit(solution)/shard_map/pallas_call | solution.py:64
  72.6 2.7 %shard_map.168.near_ref = f32[3,768,288]{2,1,0:T(8,128)S(1)} custom-call(bf16[256,768]{1,0:T(8,128)(2,1)} %get-tuple-element.80.near_ref.n0, bf16[256,768]{1,0:T(8,128)(2,1)} %collective-permute-done.9.far_ref.n1, bf16[256,768]{1,0:T(8,128)(2,1)S(1)} %copy-done.6, bf16[256,768]{1,0:T(8,128)(2,1)} %collective-permute-done.10.grad_far_ref.g1, ...), custom_call_target="tpu_custom_call" | custom-call | flops 679477248 | bytes 2457600 | tf_op jit(solution)/shard_map/pallas_call | solution.py:64
  77.2 4.6 %shard_map.159 = (bf16[512,288]{1,0:T(8,128)(2,1)S(1)}, bf16[512,288]{1,0:T(8,128)(2,1)S(1)}, bf16[512,288]{1,0:T(8,128)(2,1)S(1)}, f32[256,768]{1,0:T(8,128)S(1...) custom-call(bf16[256,768]{1,0:T(8,128)(2,1)} %collective-permute-done.11.near_ref.n0, ...), custom_call_target="tpu_custom_call" | custom-call | flops 1358954496 | bytes 2899968 | tf_op jit(solution)/shard_map/pallas_call | solution.py:64
  84.0 6.0 %shard_map.169 = (f32[4,48,864]{2,1,0:T(8,128)}, bf16[4,48,864]{2,1,0:T(8,128)(2,1)}, f32[4,48,864]{2,1,0:T(8,128)}, bf16[4,48,864]{2,1,0:T(8,128)(2,1)}) custom-call(s32[1]{0:T(128)} %bitcast.10.own_ref, bf16[256,768]{1,0:T(8,128)(2,1)} %collective-permute-done.11.near_ref.n0, bf16[256,768]{1,0:T(8,128)(2,1)} %copy-done.10, bf16[256,768]{1,0:T(8,128)(2,1)} %copy-done.8, ...), custom_call_target="tpu_custom_call" | custom-call | flops 679477248 | bytes 5111812 | tf_op jit(solution)/shard_map/pallas_call | solution.py:64
  95.8 4.7 %collective-permute-done.36 = bf16[4,48,864]{2,1,0:T(8,128)(2,1)S(1)} collective-permute-done((bf16[4,48,864]{2,1,0:T(8,128)(2,1)}, bf16[4,48,864]{2,1,0:T(8,128)(2,1)S(1)}, u32[]{:S(2)}, u32[]{:S(2)}) %collective-permute-start.36) | collective-permute-done | bytes 331808 | tf_op jit(solution)/shard_map/ppermute | solution.py:29
  101.8 1.9 collective-permute-start.37
  105.5 2.6 %collective-permute-start.40 = (bf16[2,48,864]{2,1,0:T(8,128)(2,1)S(1)}, bf16[2,48,864]{2,1,0:T(8,128)(2,1)S(1)}, u32[]{:S(2)}, u32[]{:S(2)}) collective-permute-start(bf16[2,48,864]{2,1,0:T(8,128)(2,1)S(1)} %slice.122), channel_id=1, source_target_pairs={{0,16},{4,20},{8,24},{12,28},{16,0},{20,4},{24,8},{28,12},{1,17},{... | collective-permute-start | bytes 497672 | tf_op jit(solution)/shard_map/ppermute | solution.py:29
  108.2 6.8 %collective-permute-done.20.chip_ref = bf16[256,768]{1,0:T(8,128)(2,1)S(1)} collective-permute-done((bf16[256,768]{1,0:T(8,128)(2,1)S(1)}, bf16[256,768]{1,0:T(8,128)(2,1)S(1)}, u32[]{:S(2)}, u32[]{:S(2)}) %collective-permute-start.20) | collective-permute-done | bytes 393248 | tf_op jit(solution)/shard_map/ppermute | solution.py:29
  119.8 2.3 %collective-permute-done.22.g2 = bf16[192,256]{1,0:T(8,128)(2,1)S(1)} collective-permute-done((bf16[192,256]{1,0:T(8,128)(2,1)S(1)}, bf16[192,256]{1,0:T(8,128)(2,1)S(1)}, u32[]{:S(2)}, u32[]{:S(2)}) %collective-permute-start.22) | collective-permute-done | bytes 98336 | tf_op jit(solution)/shard_map/ppermute | solution.py:29
  123.3 12.0 %shard_map.163 = (bf16[576,1024]{1,0:T(8,128)(2,1)S(1)}, f32[256,768]{1,0:T(8,128)S(1)}, f32[256,768]{1,0:T(8,128)S(1)}, bf16[256,768]{1,0:T(8,128)(2,1)S(1)}, b...) custom-call(bf16[576,512]{1,0:T(8,128)(2,1)S(1)} %copy-done.32, bf16[576,512]{1,0:T(8,128)(2,1)S(1)} %copy-done.34, ...), custom_call_target="tpu_custom_call" | custom-call | flops 8053063680 | bytes 5226496 | tf_op jit(solution)/shard_map/pallas_call | solution.py:64
  142.5 2.0 %collective-permute-done.44 = f32[2,768]{1,0:T(2,128)S(1)} collective-permute-done((f32[2,768]{1,0:T(2,128)S(1)}, f32[2,768]{1,0:T(2,128)S(1)}, u32[]{:S(2)}, u32[]{:S(2)}) %collective-permute-start.44) | collective-permute-done | bytes 6176 | tf_op jit(solution)/shard_map/ppermute | solution.py:29
  148.2 2.7 %collective-permute-start.38 = (bf16[48,864]{1,0:T(8,128)(2,1)S(1)}, bf16[48,864]{1,0:T(8,128)(2,1)S(1)}, u32[]{:S(2)}, u32[]{:S(2)}) collective-permute-start(bf16[48,864]{1,0:T(8,128)(2,1)S(1)} %fusion.4), channel_id=1, source_target_pairs={{0,16},{4,20},{8,24},{12,28},{16,0},{20,4},{24,8},{28,12},{1,17},{... | collective-permute-start | bytes 248840 | tf_op jit(solution)/shard_map/ppermute | solution.py:29
  155.8 2.0 %collective-permute-start.46 = (f32[2,768]{1,0:T(2,128)S(1)}, f32[2,768]{1,0:T(2,128)S(1)}, u32[]{:S(2)}, u32[]{:S(2)}) collective-permute-start(f32[2,768]{1,0:T(2,128)S(1)} %add.70), channel_id=1, source_target_pairs={{0,16},{4,20},{8,24},{12,28},{16,0},{20,4},{24,8},{28,12},{1,17},{... | collective-permute-start | bytes 18440 | tf_op jit(solution)/shard_map/ppermute | solution.py:29
  163.8 1.8 collective-permute-start.33
  167.4 6.3 %collective-permute-done.33 = bf16[4,96,384]{2,1,0:T(8,128)(2,1)S(1)} collective-permute-done((bf16[4,96,384]{2,1,0:T(8,128)(2,1)S(1)}, bf16[4,96,384]{2,1,0:T(8,128)(2,1)S(1)}, u32[]{:S(2)}, u32[]{:S(2)}) %collective-permute-start.33) | collective-permute-done | bytes 294944 | tf_op jit(solution)/shard_map/ppermute | solution.py:29
  178.4 6.4 %collective-permute-done.34 = bf16[2,96,384]{2,1,0:T(8,128)(2,1)S(1)} collective-permute-done((bf16[2,96,384]{2,1,0:T(8,128)(2,1)S(1)}, bf16[2,96,384]{2,1,0:T(8,128)(2,1)S(1)}, u32[]{:S(2)}, u32[]{:S(2)}) %collective-permute-start.34) | collective-permute-done | bytes 147488 | tf_op jit(solution)/shard_map/ppermute | solution.py:29
  185.9 3.4 %collective-permute-done.35.came_b = bf16[96,384]{1,0:T(8,128)(2,1)S(1)} collective-permute-done((bf16[96,384]{1,0:T(8,128)(2,1)S(1)}, bf16[96,384]{1,0:T(8,128)(2,1)S(1)}, u32[]{:S(2)}, u32[]{:S(2)}) %collective-permute-start.35) | collective-permute-done | bytes 73760 | tf_op jit(solution)/shard_map/ppermute | solution.py:29
  (214 shorter events, 74.9 us)
Async XLA Ops:
  0.6 12.4 %collective-permute-start.1 = (bf16[256,768]{1,0:T(8,128)(2,1)}, bf16[256,768]{1,0:T(8,128)(2,1)S(1)}, u32[]{:S(2)}, u32[]{:S(2)}) collective-permute-start(bf16[256,768]{1,0:T(8,128)(2,1)} %x_ref.3), channel_id=1, source_target_pairs={{0,2},{1,3},{2,0},{3,1},{4,6},{5,7},{6,4},{7,5},{8,10},{9,11},{10,... | collective-permute-start | bytes 1179656 | tf_op jit(solution)/shard_map/ppermute | solution.py:29
  3.7 19.0 %collective-permute-start = (bf16[256,768]{1,0:T(8,128)(2,1)}, bf16[256,768]{1,0:T(8,128)(2,1)S(1)}, u32[]{:S(2)}, u32[]{:S(2)}) collective-permute-start(bf16[256,768]{1,0:T(8,128)(2,1)} %x_ref.3), channel_id=1, source_target_pairs={{0,1},{1,0},{2,3},{3,2},{4,5},{5,4},{6,7},{7,6},{8,9},{9,8},{10,11... | collective-permute-start | bytes 1179656 | tf_op jit(solution)/shard_map/ppermute | solution.py:29
  13.0 14.7 %collective-permute-start.2 = (bf16[256,768]{1,0:T(8,128)(2,1)S(1)}, bf16[256,768]{1,0:T(8,128)(2,1)S(1)}, u32[]{:S(2)}, u32[]{:S(2)}) collective-permute-start(bf16[256,768]{1,0:T(8,128)(2,1)S(1)} %collective-permute-done.1.near_ref), channel_id=1, source_target_pairs={{0,1},{1,0},{2,3},{3,2},{4,5},{5,4},{6,7},{7,6},{8,9},{9,8},{10,11... | collective-permute-start | bytes 1179656 | tf_op jit(solution)/shard_map/ppermute | solution.py:29
  14.7 28.8 %collective-permute-start.6 = (bf16[192,768]{1,0:T(8,128)(2,1)}, bf16[192,768]{1,0:T(8,128)(2,1)S(1)}, u32[]{:S(2)}, u32[]{:S(2)}) collective-permute-start(bf16[192,768]{1,0:T(8,128)(2,1)} %w0.3), channel_id=1, source_target_pairs={{0,1},{1,0},{2,3},{3,2},{4,5},{5,4},{6,7},{7,6},{8,9},{9,8},{10,11... | collective-permute-start | bytes 884744 | tf_op jit(solution)/shard_map/ppermute | solution.py:29
  22.6 22.3 %collective-permute-start.8 = (bf16[192,768]{1,0:T(8,128)(2,1)S(1)}, bf16[192,768]{1,0:T(8,128)(2,1)S(1)}, u32[]{:S(2)}, u32[]{:S(2)}) collective-permute-start(bf16[192,768]{1,0:T(8,128)(2,1)S(1)} %collective-permute-done.7.w2), channel_id=1, source_target_pairs={{0,1},{1,0},{2,3},{3,2},{4,5},{5,4},{6,7},{7,6},{8,9},{9,8},{10,11... | collective-permute-start | bytes 884744 | tf_op jit(solution)/shard_map/ppermute | solution.py:29
  43.6 13.7 %collective-permute-start.13 = (bf16[256,768]{1,0:T(8,128)(2,1)S(1)}, bf16[256,768]{1,0:T(8,128)(2,1)S(1)}, u32[]{:S(2)}, u32[]{:S(2)}) collective-permute-start(bf16[256,768]{1,0:T(8,128)(2,1)S(1)} %copy-done.6), channel_id=1, source_target_pairs={{0,2},{1,3},{2,0},{3,1},{4,6},{5,7},{6,4},{7,5},{8,10},{9,11},{10,... | collective-permute-start | bytes 1179656 | tf_op jit(solution)/shard_map/ppermute | solution.py:29
  50.4 15.1 %collective-permute-start.11 = (bf16[256,768]{1,0:T(8,128)(2,1)}, bf16[256,768]{1,0:T(8,128)(2,1)}, u32[]{:S(2)}, u32[]{:S(2)}) collective-permute-start(bf16[256,768]{1,0:T(8,128)(2,1)} %get-tuple-element.80.near_ref.n0), channel_id=1, source_target_pairs={{0,2},{1,3},{2,0},{3,1},{4,6},{5,7},{6,4},{7,5},{8,10},{9,11},{10,... | collective-permute-start | bytes 1179656 | tf_op jit(solution)/shard_map/ppermute | solution.py:29
  50.9 15.9 %collective-permute-start.10 = (bf16[256,768]{1,0:T(8,128)(2,1)S(1)}, bf16[256,768]{1,0:T(8,128)(2,1)}, u32[]{:S(2)}, u32[]{:S(2)}) collective-permute-start(bf16[256,768]{1,0:T(8,128)(2,1)S(1)} %copy-done.6), channel_id=1, source_target_pairs={{0,1},{1,0},{2,3},{3,2},{4,5},{5,4},{6,7},{7,6},{8,9},{9,8},{10,11... | collective-permute-start | bytes 1179656 | tf_op jit(solution)/shard_map/ppermute | solution.py:29
  52.4 14.5 %collective-permute-start.9 = (bf16[256,768]{1,0:T(8,128)(2,1)}, bf16[256,768]{1,0:T(8,128)(2,1)}, u32[]{:S(2)}, u32[]{:S(2)}) collective-permute-start(bf16[256,768]{1,0:T(8,128)(2,1)} %get-tuple-element.80.near_ref.n0), channel_id=1, source_target_pairs={{0,1},{1,0},{2,3},{3,2},{4,5},{5,4},{6,7},{7,6},{8,9},{9,8},{10,11... | collective-permute-start | bytes 1179656 | tf_op jit(solution)/shard_map/ppermute | solution.py:29
  57.2 19.9 %collective-permute-start.14 = (bf16[256,768]{1,0:T(8,128)(2,1)S(1)}, bf16[256,768]{1,0:T(8,128)(2,1)S(1)}, u32[]{:S(2)}, u32[]{:S(2)}) collective-permute-start(bf16[256,768]{1,0:T(8,128)(2,1)S(1)} %collective-permute-done.13.grad_near_ref.g0), channel_id=1, source_target_pairs={{0,1},{1,0},{2,3},{3,2},{4,5},{5,4},{6,7},{7,6},{8,9},{9,8},{10,11... | collective-permute-start | bytes 1179656 | tf_op jit(solution)/shard_map/ppermute | solution.py:29
  65.5 11.6 %collective-permute-start.12 = (bf16[256,768]{1,0:T(8,128)(2,1)}, bf16[256,768]{1,0:T(8,128)(2,1)S(1)}, u32[]{:S(2)}, u32[]{:S(2)}) collective-permute-start(bf16[256,768]{1,0:T(8,128)(2,1)} %collective-permute-done.11.near_ref.n0), channel_id=1, source_target_pairs={{0,1},{1,0},{2,3},{3,2},{4,5},{5,4},{6,7},{7,6},{8,9},{9,8},{10,11... | collective-permute-start | bytes 1179656 | tf_op jit(solution)/shard_map/ppermute | solution.py:29
  90.0 10.6 %collective-permute-start.36 = (bf16[4,48,864]{2,1,0:T(8,128)(2,1)}, bf16[4,48,864]{2,1,0:T(8,128)(2,1)S(1)}, u32[]{:S(2)}, u32[]{:S(2)}) collective-permute-start(bf16[4,48,864]{2,1,0:T(8,128)(2,1)} %get-tuple-element.123), channel_id=1, source_target_pairs={{0,4},{4,0},{8,12},{12,8},{16,20},{20,16},{24,28},{28,24},{1,5},{5... | collective-permute-start | bytes 995336 | tf_op jit(solution)/shard_map/ppermute | solution.py:29
  91.6 16.6 %collective-permute-start.18 = (bf16[256,768]{1,0:T(8,128)(2,1)}, bf16[256,768]{1,0:T(8,128)(2,1)S(1)}, u32[]{:S(2)}, u32[]{:S(2)}) collective-permute-start(bf16[256,768]{1,0:T(8,128)(2,1)} %get-tuple-element.88), channel_id=1, source_target_pairs={{0,1},{1,0},{2,3},{3,2},{4,5},{5,4},{6,7},{7,6},{8,9},{9,8},{10,11... | collective-permute-start | bytes 1179656 | tf_op jit(solution)/shard_map/ppermute | solution.py:29
  92.1 11.6 %collective-permute-start.39 = (bf16[4,48,864]{2,1,0:T(8,128)(2,1)}, bf16[4,48,864]{2,1,0:T(8,128)(2,1)S(1)}, u32[]{:S(2)}, u32[]{:S(2)}) collective-permute-start(bf16[4,48,864]{2,1,0:T(8,128)(2,1)} %get-tuple-element.125), channel_id=1, source_target_pairs={{0,8},{4,12},{8,0},{12,4},{16,24},{20,28},{24,16},{28,20},{1,9},{5... | collective-permute-start | bytes 995336 | tf_op jit(solution)/shard_map/ppermute | solution.py:29
  95.7 64.9 %collective-permute-start.15 = (bf16[256,768]{1,0:T(8,128)(2,1)S(1)}, bf16[256,768]{1,0:T(8,128)(2,1)S(1)}, u32[]{:S(2)}, u32[]{:S(2)}) collective-permute-start(bf16[256,768]{1,0:T(8,128)(2,1)S(1)} %get-tuple-element.84), channel_id=1, source_target_pairs={{0,1},{1,0},{2,3},{3,2},{4,5},{5,4},{6,7},{7,6},{8,9},{9,8},{10,11... | collective-permute-start | bytes 1179656 | tf_op jit(solution)/shard_map/ppermute | solution.py:29
  101.8 16.1 %collective-permute-start.37 = (bf16[2,48,864]{2,1,0:T(8,128)(2,1)S(1)}, bf16[2,48,864]{2,1,0:T(8,128)(2,1)S(1)}, u32[]{:S(2)}, u32[]{:S(2)}) collective-permute-start(bf16[2,48,864]{2,1,0:T(8,128)(2,1)S(1)} %fusion.2), channel_id=1, source_target_pairs={{0,8},{4,12},{8,0},{12,4},{16,24},{20,28},{24,16},{28,20},{1,9},{5... | collective-permute-start | bytes 497672 | tf_op jit(solution)/shard_map/ppermute | solution.py:29
  103.7 11.3 %collective-permute-start.20 = (bf16[256,768]{1,0:T(8,128)(2,1)S(1)}, bf16[256,768]{1,0:T(8,128)(2,1)S(1)}, u32[]{:S(2)}, u32[]{:S(2)}) collective-permute-start(bf16[256,768]{1,0:T(8,128)(2,1)S(1)} %add_convert_fusion.1), channel_id=1, source_target_pairs={{0,2},{1,3},{2,0},{3,1},{4,6},{5,7},{6,4},{7,5},{8,10},{9,11},{10,... | collective-permute-start | bytes 1179656 | tf_op jit(solution)/shard_map/ppermute | solution.py:29
  105.5 30.8 %collective-permute-start.40 = (bf16[2,48,864]{2,1,0:T(8,128)(2,1)S(1)}, bf16[2,48,864]{2,1,0:T(8,128)(2,1)S(1)}, u32[]{:S(2)}, u32[]{:S(2)}) collective-permute-start(bf16[2,48,864]{2,1,0:T(8,128)(2,1)S(1)} %slice.122), channel_id=1, source_target_pairs={{0,16},{4,20},{8,24},{12,28},{16,0},{20,4},{24,8},{28,12},{1,17},{... | collective-permute-start | bytes 497672 | tf_op jit(solution)/shard_map/ppermute | solution.py:29
  118.2 42.4 %collective-permute-start.17 = (bf16[256,768]{1,0:T(8,128)(2,1)S(1)}, bf16[256,768]{1,0:T(8,128)(2,1)S(1)}, u32[]{:S(2)}, u32[]{:S(2)}) collective-permute-start(bf16[256,768]{1,0:T(8,128)(2,1)S(1)} %add_convert_fusion.2), channel_id=1, source_target_pairs={{0,2},{1,3},{2,0},{3,1},{4,6},{5,7},{6,4},{7,5},{8,10},{9,11},{10,... | collective-permute-start | bytes 1179656 | tf_op jit(solution)/shard_map/ppermute | solution.py:29
  148.1 14.0 %collective-permute-start.25 = (bf16[256,768]{1,0:T(8,128)(2,1)S(1)}, bf16[256,768]{1,0:T(8,128)(2,1)S(1)}, u32[]{:S(2)}, u32[]{:S(2)}) collective-permute-start(bf16[256,768]{1,0:T(8,128)(2,1)S(1)} %get-tuple-element.103), channel_id=1, source_target_pairs={{0,1},{1,0},{2,3},{3,2},{4,5},{5,4},{6,7},{7,6},{8,9},{9,8},{10,11... | collective-permute-start | bytes 1179656 | tf_op jit(solution)/shard_map/ppermute | solution.py:29
  161.5 14.0 %collective-permute-start.24 = (bf16[256,768]{1,0:T(8,128)(2,1)S(1)}, bf16[256,768]{1,0:T(8,128)(2,1)S(1)}, u32[]{:S(2)}, u32[]{:S(2)}) collective-permute-start(bf16[256,768]{1,0:T(8,128)(2,1)S(1)} %get-tuple-element.101), channel_id=1, source_target_pairs={{0,1},{1,0},{2,3},{3,2},{4,5},{5,4},{6,7},{7,6},{8,9},{9,8},{10,11... | collective-permute-start | bytes 1179656 | tf_op jit(solution)/shard_map/ppermute | solution.py:29
  162.2 13.3 %collective-permute-start.26 = (bf16[256,768]{1,0:T(8,128)(2,1)S(1)}, bf16[256,768]{1,0:T(8,128)(2,1)S(1)}, u32[]{:S(2)}, u32[]{:S(2)}) collective-permute-start(bf16[256,768]{1,0:T(8,128)(2,1)S(1)} %add_convert_fusion), channel_id=1, source_target_pairs={{0,2},{1,3},{2,0},{3,1},{4,6},{5,7},{6,4},{7,5},{8,10},{9,11},{10,... | collective-permute-start | bytes 1179656 | tf_op jit(solution)/shard_map/ppermute | solution.py:29
  165.7 11.4 %collective-permute-start.31 = (bf16[2,96,384]{2,1,0:T(8,128)(2,1)S(1)}, bf16[2,96,384]{2,1,0:T(8,128)(2,1)S(1)}, u32[]{:S(2)}, u32[]{:S(2)}) collective-permute-start(bf16[2,96,384]{2,1,0:T(8,128)(2,1)S(1)} %fusion.3), channel_id=1, source_target_pairs={{0,8},{4,12},{8,0},{12,4},{16,24},{20,28},{24,16},{28,20},{1,9},{5... | collective-permute-start | bytes 442376 | tf_op jit(solution)/shard_map/ppermute | solution.py:29
  173.8 11.0 %collective-permute-start.34 = (bf16[2,96,384]{2,1,0:T(8,128)(2,1)S(1)}, bf16[2,96,384]{2,1,0:T(8,128)(2,1)S(1)}, u32[]{:S(2)}, u32[]{:S(2)}) collective-permute-start(bf16[2,96,384]{2,1,0:T(8,128)(2,1)S(1)} %slice.123), channel_id=1, source_target_pairs={{0,16},{4,20},{8,24},{12,28},{16,0},{20,4},{24,8},{28,12},{1,17},{... | collective-permute-start | bytes 442376 | tf_op jit(solution)/shard_map/ppermute | solution.py:29
  (68 other events, 537.6 us)
